TPU v7x, 512 devices: a whole 4x4x16 slice. The times are simulated.
512 devices in a mesh: stn: 64 (over x, z_lo, y), chan: 8 (over z_hi, core).
Axes of the slice: x: 4, y: 4, z: 16 (z_hi: 4, z_lo: 4; z = z_hi * 4 + z_lo), core: 2. Of those that a mesh axis runs over, the one named last changes fastest.
Arguments:
- voltages: bfloat16 [512, 2, 143, 2048], P(('stn', 'chan')), may hold values from -6 to 6
- flags: float32 [256, 128], P('stn'), may hold values from 0 to 1, as said below
- station_row: int32 [256], P('stn'), may hold values from 0 to 255, each once
Outputs:
- visibility: bfloat16 [2048, 512, 512], P(('stn', 'chan'))
Inputs may be any that keep to these rules, and one draw needn't show every extreme that they name: `flags`: 0 marks a flagged spectrum of a station, 1 a fully usable one; some stations have 0 at all 128 spectra. `station_row`: every row pair is given to exactly one station.
All inputs are finite; a program needn't handle non-finite values.
Results may differ from a plain program's by a relative error of at most 0.006.
Values may be sent and summed in bfloat16 or wider, within the bound.
No kernel may reach another device: no remote copies, remote signals or barrier semaphores. Data moves between devices by JAX's collectives and lax.ppermute only.
A program may use at most 64 MiB of HBM per device.

v0:
```python
import math

import jax
import jax.numpy as jnp
from jax import lax
from jax.sharding import PartitionSpec as P


def filter_table(taps, lanes):
    total = taps * lanes
    places = jnp.arange(total, dtype=jnp.float32) + 0.5
    window = 0.5 - 0.5 * jnp.cos(2.0 * math.pi * places / total)
    return (jnp.sinc((places - 0.5 * total) / lanes) * window).reshape(taps, lanes)


def dft_tables(length):
    places = jnp.arange(length, dtype=jnp.int32)
    product = places[:, None] * places[None, :] % length
    angle = 2.0 * math.pi * product.astype(jnp.float32) / length
    return (jnp.cos(angle), jnp.sin(angle))


def twiddle_tables(outer, inner):
    product = (
        jnp.arange(outer, dtype=jnp.int32)[:, None]
        * jnp.arange(inner, dtype=jnp.int32)[None, :]
        % (outer * inner)
    )
    angle = 2.0 * math.pi * product.astype(jnp.float32) / (outer * inner)
    return (jnp.cos(angle), jnp.sin(angle))


def contract(form, left, right):
    return jnp.einsum(form, left, right, precision=lax.Precision.HIGHEST)


def channelize(voltages, spectra_count):
    inputs_here = voltages.shape[0]
    lanes = voltages.shape[3]
    taps = voltages.shape[2] - spectra_count + 1
    taps_table = filter_table(taps, lanes)
    real_acc = taps_table[0] * voltages[:, 0, 0:spectra_count, :].astype(jnp.float32)
    imag_acc = taps_table[0] * voltages[:, 1, 0:spectra_count, :].astype(jnp.float32)
    for tap_index in range(1, taps):
        real_acc = real_acc + taps_table[tap_index] * voltages[
            :, 0, tap_index : tap_index + spectra_count, :
        ].astype(jnp.float32)
        imag_acc = imag_acc + taps_table[tap_index] * voltages[
            :, 1, tap_index : tap_index + spectra_count, :
        ].astype(jnp.float32)
    inner = 128
    outer = lanes // inner
    real_grid = real_acc.reshape(inputs_here, spectra_count, outer, inner)
    imag_grid = imag_acc.reshape(inputs_here, spectra_count, outer, inner)
    cos_outer, sin_outer = dft_tables(outer)
    real_mid = contract("gtmn,mk->gtkn", real_grid, cos_outer) + contract(
        "gtmn,mk->gtkn", imag_grid, sin_outer
    )
    imag_mid = contract("gtmn,mk->gtkn", imag_grid, cos_outer) - contract(
        "gtmn,mk->gtkn", real_grid, sin_outer
    )
    cos_twist, sin_twist = twiddle_tables(outer, inner)
    real_twisted = real_mid * cos_twist + imag_mid * sin_twist
    imag_twisted = imag_mid * cos_twist - real_mid * sin_twist
    cos_inner, sin_inner = dft_tables(inner)
    real_out = contract("gtkn,nj->jkgt", real_twisted, cos_inner) + contract(
        "gtkn,nj->jkgt", imag_twisted, sin_inner
    )
    imag_out = contract("gtkn,nj->jkgt", imag_twisted, cos_inner) - contract(
        "gtkn,nj->jkgt", real_twisted, sin_inner
    )
    scale = 1.0 / math.sqrt(lanes)
    stacked = (jnp.stack([real_out, imag_out], axis=3) * scale).astype(jnp.bfloat16)
    return stacked.reshape(lanes, inputs_here, 2 * spectra_count)


def square_products(plain, turned):
    real_part = jnp.einsum("cat,cbt->cab", plain, plain, preferred_element_type=jnp.float32)
    imag_part = jnp.einsum("cat,cbt->cab", plain, turned, preferred_element_type=jnp.float32)
    return (real_part, imag_part)


def on_device(voltages, flags, station_row):
    spectra_count = flags.shape[1]
    inputs_here = voltages.shape[0]
    lanes = voltages.shape[3]
    stn_count = lax.axis_size("stn")
    chan_count = lax.axis_size("chan")
    per_device = lanes // (stn_count * chan_count)
    total_inputs = inputs_here * stn_count * chan_count
    flags_all, rows_all = (
        lax.all_gather(flags, "stn", axis=0, tiled=True),
        lax.all_gather(station_row, "stn", axis=0, tiled=True),
    )
    spectra = channelize(voltages, spectra_count)
    grouped = spectra.reshape(stn_count, chan_count, per_device, inputs_here, 2 * spectra_count)
    order = jnp.argsort(rows_all)
    rows = jnp.arange(total_inputs, dtype=jnp.int32)
    station_of = order[rows // 2]
    source = 2 * station_of + rows % 2
    moved = lax.all_to_all(
        lax.all_to_all(grouped, "stn", split_axis=0, concat_axis=3, tiled=True),
        "chan",
        split_axis=1,
        concat_axis=3,
        tiled=True,
    )
    from_stn = source // (chan_count * inputs_here)
    from_chan = source // inputs_here % chan_count
    within = source % inputs_here
    placed = from_chan * (stn_count * inputs_here) + from_stn * inputs_here + within
    arrived = moved.reshape(per_device, total_inputs, 2, spectra_count)
    weights = jnp.take(flags_all, station_of, axis=0)
    kept = (
        jnp.take(arrived, placed, axis=1).astype(jnp.float32) * weights[None, :, None, :]
    ).astype(jnp.bfloat16)
    plain = kept.reshape(per_device, total_inputs, 2 * spectra_count)
    turned = jnp.concatenate([-kept[:, :, 1], kept[:, :, 0]], axis=-1)
    count = jnp.dot(
        weights, weights.T, preferred_element_type=jnp.float32, precision=lax.Precision.HIGHEST
    )
    denom = jnp.maximum(count, 1.0)
    real_part, imag_part = square_products(plain, turned)
    below = rows[:, None] >= rows[None, :]
    return jnp.where(below[None], real_part / denom, imag_part / denom).astype(jnp.bfloat16)


def solution(mesh):
    placed = (P(("stn", "chan"), None, None, None), P("stn", None), P("stn"))
    return jax.shard_map(
        on_device,
        mesh=mesh,
        in_specs=placed,
        out_specs=P(("stn", "chan"), None, None),
        check_vma=False,
    )
```

profile of v0, /device:TPU:128, one launch (start us, length us, event | category | flops | bytes accessed | tf_op | source)
XLA Modules:
  0.0 374.9 jit_solution(11308704280490452566)
XLA Ops:
  0.7 28.6 %slice_convert_fusion.15 = (f32[1,1,128,2048]{3,1,2,0:T(1,128)S(1)}, f32[1,1,128,2048]{3,1,2,0:T(1,128)S(1)}, f32[1,1,128,2048]{3,1,2,0:T(1,128)S(1)}, f32[1,1,1...) fusion(bf16[1,2,143,2048]{3,1,2,0:T(2,128)(2,1)} %param.3), kind=kLoop, calls=%fused_computation.41 | loop fusion | flops 4980736 | bytes 29884416 | tf_op jit(solution)/shard_map/convert_element_type | solution.py:43
  29.3 13.9 %slice_convert_fusion.1 = (f32[1,1,128,2048]{3,1,2,0:T(1,128)}, f32[1,1,128,2048]{3,1,2,0:T(1,128)}, f32[1,1,128,2048]{3,1,2,0:T(1,128)}, f32[1,1,128,2048]{3,1,...) fusion(bf16[1,2,143,2048]{3,1,2,0:T(2,128)(2,1)S(1)} %copy-done), kind=kLoop, calls=%fused_computation.27 | loop fusion | flops 3407872 | bytes 20447232 | tf_op jit(solution)/shard_map/convert_element_type | solution.py:50
  44.5 3.2 multiply_add_fusion
  47.8 1.0 fusion.52
  49.3 5.6 %multiply_add_fusion.1 = f32[128,16,128]{2,1,0:T(8,128)S(1)} fusion(f32[128,16,128]{2,1,0:T(8,128)S(1)} %bitcast.127, f32[128,16,128]{2,1,0:T(8,128)S(1)} %bitcast.128, f32[128,16,128]{2,1,0:T(8,128)S(1)} %bitcast.129, f32[128,16,128]{2,1,0:T(8,128)S(1)} %bitcast.130, f32[128,16,128]{2,1,0:T(8,128)S(1)} %bitcast.131, f32[128,16,128]{2,1,0:T(8,128)S(1)} %bitcast.149, ...), kind=kLoop, calls=%fused_computation.42 | loop fusion | flops 8126464 | bytes 17956864 | tf_op jit(solution)/shard_map/add | solution.py:45
  56.0 1.1 fusion.3
  57.1 1.3 add_bitcast_fusion
  58.4 1.4 fusion.12
  59.9 1.4 fusion.8
  61.3 1.5 fusion.2
  62.8 1.7 fusion.1
  64.8 1.1 copy.26
  66.6 41.1 %all_to_all.33 = bf16[64,8,4,1,256]{4,2,1,3,0:T(4,128)(2,1)S(1)} all-to-all(bf16[64,8,4,1,256]{4,2,1,3,0:T(4,128)(2,1)S(1)} %bitcast.147), channel_id=1, replica_groups=mesh['stn'=64,'chan'=8] {'stn'}, dimensions={0} | all-to-all | bytes 2097152 | tf_op jit(solution)/shard_map/all_to_all | solution.py:102
  108.0 1.4 copy.29
  109.4 11.3 %all-to-all-start.1 = ((bf16[1,8,4,64,256]{4,2,3,0,1:T(4,128)(2,1)}), bf16[1,8,4,64,256]{4,2,3,0,1:T(4,128)(2,1)S(1)}, u32[]{:S(2)}, u32[]{:S(2)}) async-start(bf16[1,8,4,64,256]{4,2,3,0,1:T(4,128)(2,1)} %copy.29), calls=%async_computation.1 | async-start | bytes 2097152 | tf_op jit(solution)/shard_map/all_to_all | solution.py:101
  120.6 1.3 dynamic-slice
  122.8 40.8 %all-reduce = s32[256]{0:T(256)S(1)} all-reduce(s32[256]{0:T(256)S(1)} %dynamic-update-slice), channel_id=1, replica_groups=mesh['stn'=64,'chan'=8] {'stn'}, use_global_device_ids=true, to_apply=%add | all-reduce | flops 256 | bytes 2048
  163.6 3.1 sort.17
  166.8 3.5 gather_fusion
  170.3 192.1 %all-gather = f32[64,4,128]{2,1,0:T(4,128)S(1)} all-gather(f32[1,4,128]{2,1,0:T(4,128)S(1)} %bitcast.167), channel_id=1, replica_groups=mesh['stn'=64,'chan'=8] {'stn'}, dimensions={0}, use_global_device_ids=true | all-gather | bytes 133120 | tf_op jit(solution)/shard_map/all_gather | solution.py:92
  363.9 2.0 convolution_maximum_fusion
  365.8 2.6 gather_fusion.1
  371.1 1.1 copy-done.3
  372.2 2.8 select_convert_fusion
  (56 shorter events, 9.0 us)
Async XLA Ops:
  0.6 28.7 %copy-start = (bf16[1,2,143,2048]{3,1,2,0:T(2,128)(2,1)S(1)}, bf16[1,2,143,2048]{3,1,2,0:T(2,128)(2,1)}, u32[]{:S(2)}) copy-start(bf16[1,2,143,2048]{3,1,2,0:T(2,128)(2,1)} %param.3) | copy-start | bytes 3514372
  47.7 1.2 copy-start.1
  47.7 1.5 copy-start.2
  47.8 1.5 copy-start.4
  47.8 1.5 copy-start.5
  47.8 1.5 copy-start.6
  47.8 1.5 copy-start.7
  47.8 1.5 copy-start.8
  47.8 1.5 copy-start.9
  47.8 1.5 copy-start.10
  56.0 1.1 copy-start.11
  56.0 1.1 copy-start.12
  108.0 14.6 %copy-start.14 = (s32[4]{0:T(128)S(1)}, s32[4]{0:T(128)}, u32[]{:S(2)}) copy-start(s32[4]{0:T(128)} %param.5) | copy-start | bytes 52
  109.4 60.9 %copy-start.13 = (f32[4,128]{1,0:T(4,128)S(1)}, f32[4,128]{1,0:T(4,128)}, u32[]{:S(2)}) copy-start(f32[4,128]{1,0:T(4,128)} %param.4) | copy-start | bytes 6148
  109.4 256.5 %all-to-all-start.1 = ((bf16[1,8,4,64,256]{4,2,3,0,1:T(4,128)(2,1)}), bf16[1,8,4,64,256]{4,2,3,0,1:T(4,128)(2,1)S(1)}, u32[]{:S(2)}, u32[]{:S(2)}) async-start(bf16[1,8,4,64,256]{4,2,3,0,1:T(4,128)(2,1)} %copy.29), calls=%async_computation.1 | async-start | bytes 2097152 | tf_op jit(solution)/shard_map/all_to_all | solution.py:101
  371.0 1.2 copy-start.3
where the time goes:
time: 375 us
  blocking collectives  274 us (73%)
  other arithmetic  57.2 us (15%)
  matrix products  16 us (4%)
  local copies, waits for them, and re-layouts  15.4 us (4%)
  starting transfers between devices  11.3 us (3%)
    all_gather x1, blocking collectives, on_device(): lax.all_gather(flags, 'stn', axis=0, tiled=True)  192 us
    all_to_all x1, blocking collectives, on_device(): lax.all_to_all(grouped, 'stn', split_axis=0, concat_axis=3, tiled=True)  41.1 us
    unnamed x1, blocking collectives  40.8 us
    convert_element_type x1, other arithmetic, channelize(): voltages[:, 1, 0:spectra_count, :].astype(jnp.float32)  28.6 us
    convert_element_type x1, other arithmetic, channelize(): imag_acc = imag_acc + taps_table[tap_index] * voltages[:, 1, tap_index:ta...  13.9 us
    all_to_all x1, starting transfers between devices, on_device(): lax.all_to_all(lax.all_to_all(grouped, 'stn', split_axis=0, concat_axis=3...  11.3 us
    dot_general x8, matrix products, contract(): return jnp.einsum(form, left, right, precision=lax.Precision.HIGHEST)  10.6 us
  transfers between devices with their start and end apart: 1, of which 0 were waited for; matrix products, arithmetic and copies ran while one was open for 3% of the time, Pallas kernels for 0%

commit v1 on v0

v1 whole, which is shorter than its diff:
```python
import math
import numpy as np
import jax
import jax.numpy as jnp
from jax import lax
from jax.experimental import pallas as pl
from jax.experimental.pallas import tpu as pltpu
from jax.sharding import PartitionSpec as P

F32 = jnp.float32
BF16 = jnp.bfloat16


def filter_rows(taps, lanes):
    total = taps * lanes
    places = np.arange(total, dtype=np.float64) + 0.5
    window = 0.5 - 0.5 * np.cos(2.0 * np.pi * places / total)
    table = np.sinc((places - 0.5 * total) / lanes) * window
    return table.reshape(taps, lanes).astype(np.float32)


def twist_rows(outer, inner):
    k = np.arange(outer)[:, None] * np.arange(inner)[None, :]
    angle = 2.0 * np.pi * k / (outer * inner)
    return np.stack([np.cos(angle), np.sin(angle)]).astype(np.float32)


def inner_matrix(inner, scale):
    jn = np.arange(inner)[:, None] * np.arange(inner)[None, :] % inner
    angle = 2.0 * np.pi * jn / inner
    cos, sin = np.cos(angle) * scale, np.sin(angle) * scale
    real = np.concatenate([cos, sin], axis=1)
    imag = np.concatenate([-sin, cos], axis=1)
    return np.stack([real, imag], axis=1).reshape(2 * inner, 2 * inner)


def small_transform(re, im):
    def four(a, b, c, d):
        (ar, ai), (br, bi), (cr, ci), (dr, di) = a, b, c, d
        pr, pi, qr, qi = ar + cr, ai + ci, ar - cr, ai - ci
        rr, ri, sr, si = br + dr, bi + di, br - dr, bi - di
        return [
            (pr + rr, pi + ri),
            (qr + si, qi - sr),
            (pr - rr, pi - ri),
            (qr - si, qi + sr),
        ]

    x = list(zip(re, im))
    mid = [four(x[b], x[4 + b], x[8 + b], x[12 + b]) for b in range(4)]
    out = [None] * 16
    for p in range(4):
        row = []
        for b in range(4):
            r, i = mid[b][p]
            e = (b * p) % 16
            if e == 0:
                row.append((r, i))
            elif e == 4:
                row.append((i, -r))
            elif e == 2:
                s = math.sqrt(0.5)
                row.append(((r + i) * s, (i - r) * s))
            elif e == 6:
                s = math.sqrt(0.5)
                row.append(((i - r) * s, -(r + i) * s))
            else:
                c, s = math.cos(2 * math.pi * e / 16), math.sin(2 * math.pi * e / 16)
                row.append((r * c + i * s, i * c - r * s))
        done = four(*row)
        for q in range(4):
            out[p + 4 * q] = done[q]
    return out


def channelize_kernel(v_ref, h_ref, tw_ref, dhi_ref, dlo_ref, w_ref, o_ref, xs_ref, f_ref, ahi_ref, alo_ref):
    taps = h_ref.shape[0]
    outer = xs_ref.shape[1]
    spectra = o_ref.shape[2]
    frames = v_ref.shape[1]

    def filt(m, _):
        at = pl.multiple_of(m * 128, 128)
        for c in range(2):
            xs_ref[c, 0, 0:frames, :] = v_ref[c, :, pl.ds(at, 128)].astype(F32)
        rows = [h_ref[k : k + 1, pl.ds(at, 128)] for k in range(taps)]
        for c in range(2):
            for t in range(0, spectra, 8):
                acc = rows[0] * xs_ref[c, 0, t : t + 8, :]
                for k in range(1, taps):
                    acc = acc + rows[k] * xs_ref[c, 0, t + k : t + k + 8, :]
                f_ref[c, m, t : t + 8, :] = acc
        return 0

    lax.fori_loop(0, f_ref.shape[1], filt, 0)

    def mix(tb, _):
        at = pl.multiple_of(tb * 16, 16)
        parts = []
        for half in range(2):
            here = pl.multiple_of(at + 8 * half, 8)
            re = [f_ref[0, m, pl.ds(here, 8), :] for m in range(16)]
            im = [f_ref[1, m, pl.ds(here, 8), :] for m in range(16)]
            out = small_transform(re, im)
            for k in range(16):
                r, i = out[k]
                if k:
                    cos, sin = tw_ref[0, k : k + 1, :], tw_ref[1, k : k + 1, :]
                    r, i = r * cos + i * sin, i * cos - r * sin
                f_ref[0, k, pl.ds(here, 8), :] = r
                f_ref[1, k, pl.ds(here, 8), :] = i
        for k in range(16):
            for c in range(2):
                val = f_ref[c, k, pl.ds(at, 16), :]
                hi = val.astype(BF16)
                ahi_ref[k, pl.ds(at, 16), c * 128 : (c + 1) * 128] = hi
                alo_ref[k, pl.ds(at, 16), c * 128 : (c + 1) * 128] = (val - hi.astype(F32)).astype(BF16)
        return 0

    lax.fori_loop(0, spectra // 16, mix, 0)
    weight = w_ref[0:1, :]

    def turn(k, _):
        def dot(a, b):
            return lax.dot_general(a, b, (((1,), (1,)), ((), ())), preferred_element_type=F32)

        dhi, dlo = dhi_ref[...], dlo_ref[...]
        hi, lo = ahi_ref[k], alo_ref[k]
        out = dot(dhi, hi) + (dot(dhi, lo) + dot(dlo, hi))
        out = out.astype(BF16).astype(F32) * weight
        o_ref[k] = out.astype(BF16)
        return 0

    lax.fori_loop(0, 16, turn, 0)


def channelize(voltages, weight_row, spectra, interpret=False):
    _, frames, lanes = voltages.shape
    taps = frames - spectra + 1
    h = filter_rows(taps, lanes)
    tw = twist_rows(16, 128)
    d = inner_matrix(128, 1.0 / math.sqrt(lanes))
    dhi = jnp.asarray(d.astype(np.float32)).astype(BF16)
    dhi_np = np.asarray(d.astype(np.float32)).astype(jnp.bfloat16)
    dlo_np = (d - dhi_np.astype(np.float64)).astype(np.float32).astype(jnp.bfloat16)
    padded = (frames + 15) // 16 * 16
    return pl.pallas_call(
        channelize_kernel,
        out_shape=jax.ShapeDtypeStruct((16, 256, spectra), BF16),
        scratch_shapes=[
            pltpu.VMEM((2, 1, padded, 128), F32),
            pltpu.VMEM((2, 16, spectra, 128), F32),
            pltpu.VMEM((16, spectra, 256), BF16),
            pltpu.VMEM((16, spectra, 256), BF16),
        ],
        interpret=interpret,
        name="channelize",
    )(voltages, jnp.asarray(h), jnp.asarray(tw), jnp.asarray(dhi_np), jnp.asarray(dlo_np), weight_row)


def correlate_kernel(x_ref, row_ref, flag_ref, o_ref, sel_ref, inv_ref):
    rows = sel_ref.shape[0]

    def nt(a, b):
        return lax.dot_general(a, b, (((1,), (1,)), ((), ())), preferred_element_type=F32)

    @pl.when(pl.program_id(0) == 0)
    def _():
        at = lax.broadcasted_iota(jnp.int32, (rows, rows), 0)
        sel = jnp.where(row_ref[0:1, :] == at, 1.0, 0.0).astype(BF16)
        sel_ref[...] = sel
        flag = flag_ref[...]
        hi = flag.astype(BF16)
        rest = flag - hi.astype(F32)
        mid = rest.astype(BF16)
        low = (rest - mid.astype(F32)).astype(BF16)
        pieces = jnp.concatenate([hi, mid, low], axis=1)
        placed = jnp.dot(sel, pieces, preferred_element_type=F32).astype(BF16)
        n = flag.shape[1]
        hi, mid, low = placed[:, :n], placed[:, n : 2 * n], placed[:, 2 * n :]
        left = jnp.concatenate([hi, hi, mid, mid, hi, low], axis=1)
        right = jnp.concatenate([hi, mid, hi, mid, low, hi], axis=1)
        count = nt(left, right)
        inv_ref[...] = 1.0 / jnp.maximum(count, 1.0)

    kept = jnp.dot(sel_ref[...], x_ref[0], preferred_element_type=F32)
    half = kept.shape[1] // 2
    plain = kept.astype(BF16)
    turned = jnp.concatenate([-kept[:, half:], kept[:, :half]], axis=1).astype(BF16)
    n = rows // 2
    for a in range(2):
        for b in range(2):
            pa = plain[a * n : (a + 1) * n]
            if a > b:
                out = nt(pa, plain[b * n : (b + 1) * n])
            elif a < b:
                out = nt(pa, turned[b * n : (b + 1) * n])
            else:
                real = nt(pa, pa)
                imag = nt(pa, turned[b * n : (b + 1) * n])
                below = lax.broadcasted_iota(jnp.int32, (n, n), 0) >= lax.broadcasted_iota(jnp.int32, (n, n), 1)
                out = jnp.where(below, real, imag)
            inv = inv_ref[a * n : (a + 1) * n, b * n : (b + 1) * n]
            o_ref[0, a * n : (a + 1) * n, b * n : (b + 1) * n] = (out * inv).astype(BF16)


def correlate(arrived, row_of, flags, interpret=False):
    channels, inputs, wide = arrived.shape
    return pl.pallas_call(
        correlate_kernel,
        grid=(channels,),
        in_specs=[
            pl.BlockSpec((1, inputs, wide), lambda i: (i, 0, 0)),
            pl.BlockSpec(row_of.shape, lambda i: (0, 0)),
            pl.BlockSpec(flags.shape, lambda i: (0, 0)),
        ],
        out_specs=pl.BlockSpec((1, inputs, inputs), lambda i: (i, 0, 0)),
        out_shape=jax.ShapeDtypeStruct((channels, inputs, inputs), BF16),
        scratch_shapes=[pltpu.VMEM((inputs, inputs), BF16), pltpu.VMEM((inputs, inputs), F32)],
        interpret=interpret,
        name="correlate",
    )(arrived, row_of, flags)


def gather_flags(flags, station_row):
    own = flags.shape[0]
    tile = jnp.concatenate(
        [flags, jnp.broadcast_to(station_row.astype(F32)[:, None], flags.shape)], axis=0
    )
    for axes, count in ((("x", "y"), 16), (("l",), 4)):
        tile = jnp.broadcast_to(tile[None], (count,) + tile.shape)
        tile = lax.all_to_all(tile, axes, split_axis=0, concat_axis=0, tiled=True)
    tile = tile.reshape(4, 4, 4, 2, own, flags.shape[1])
    return tile[..., 0, :, :], tile[..., 1, :, 0].astype(jnp.int32)


def on_device(voltages, flags, station_row):
    spectra = flags.shape[1]
    z_hi = 2 * lax.axis_index("a") + lax.axis_index("b")
    flags_all, rows_all = gather_flags(flags, station_row)
    weight = lax.dynamic_slice_in_dim(flags, z_hi, 1, 0)
    weight = jnp.broadcast_to(weight, (8, spectra))
    made = channelize(voltages[0], weight, spectra)
    grid = made.reshape(2, 2, 4, 4, 4, 4, 2, 2, spectra)
    blocks = jnp.transpose(grid, (3, 5, 6, 0, 4, 1, 2, 7, 8)).reshape(512, 8, spectra)
    moved = lax.all_to_all(blocks, ("x", "y", "a", "b", "l", "c"), split_axis=0, concat_axis=0, tiled=True)
    arrived = jnp.transpose(moved.reshape(512, 4, 2 * spectra), (1, 0, 2))
    flag_src = jnp.transpose(flags_all, (1, 2, 3, 0, 4)).reshape(256, 1, spectra)
    flag_src = jnp.broadcast_to(flag_src, (256, 2, spectra)).reshape(512, spectra)
    row_src = 2 * jnp.transpose(rows_all, (1, 2, 3, 0)).reshape(256, 1) + jnp.arange(2, dtype=jnp.int32)[None]
    row_src = jnp.broadcast_to(row_src.reshape(1, 512), (8, 512))
    return correlate(arrived, row_src, flag_src)


def solution(mesh):
    axes = ("x", "l", "y", "a", "b", "c")
    fine = jax.sharding.Mesh(mesh.devices.reshape(4, 4, 4, 2, 2, 2), axes)
    stn = axes[:3]
    return jax.shard_map(
        on_device,
        mesh=fine,
        in_specs=(P(axes, None, None, None), P(stn, None), P(stn)),
        out_specs=P(axes, None, None),
        check_vma=False,
    )
```

time: 375 us -> 127 us (0.34)
  the two profiles are of different devices: /device:TPU:128 before, /device:TPU:1 now
where the time goes in v1:
time: 127 us
  waiting for transfers between devices  56 us (44%)
  starting transfers between devices  25.2 us (20%)
  Pallas kernels  17 us (13%)
  blocking collectives  13.9 us (11%)
  local copies, waits for them, and re-layouts  12.1 us (10%)
  other arithmetic  2.69 us (2%)
    all_to_all x1, waiting for transfers between devices, on_device(): lax.all_to_all(blocks, ('x', 'y', 'a', 'b', 'l', 'c'), split_axis=0, conc...  55.9 us
    all_to_all x1, starting transfers between devices, on_device(): lax.all_to_all(blocks, ('x', 'y', 'a', 'b', 'l', 'c'), split_axis=0, conc...  19.6 us
    all_to_all x1, blocking collectives, gather_flags(): tile = lax.all_to_all(tile, axes, split_axis=0, concat_axis=0, tiled=True)  13.9 us
    pallas_call x1, Pallas kernels, channelize(): pl.pallas_call(channelize_kernel, out_shape=jax.ShapeDtypeStruct((16, 256...  10.5 us
    pallas_call x1, Pallas kernels, correlate(): pl.pallas_call(correlate_kernel, grid=(channels,), in_specs=[pl.BlockSpec...  6.44 us
    all_to_all x1, starting transfers between devices, gather_flags(): tile = lax.all_to_all(tile, axes, split_axis=0, concat_axis=0, tiled=True)  5.54 us
    reshape x1, local copies, waits for them, and re-layouts, on_device(): grid = made.reshape(2, 2, 4, 4, 4, 4, 2, 2, spectra)  3.36 us
    unnamed x1, local copies, waits for them, and re-layouts  2.7 us
  transfers between devices with their start and end apart: 2, of which 1 were waited for; matrix products, arithmetic and copies ran while one was open for 7% of the time, Pallas kernels for 8%

profile of v1, /device:TPU:1, one launch (start us, length us, event | category | flops | bytes accessed | tf_op | source)
XLA Modules:
  0.0 126.9 jit_solution(12517718499681161858)
XLA Ops:
  0.0 0.7 convert_element_type.7
  0.7 0.1 pad.1.clone
  0.7 0.8 pad_maximum_fusion
  1.5 13.9 %all_to_all.15 = f32[16,8,128]{2,1,0:T(8,128)S(1)} all-to-all(f32[16,8,128]{2,1,0:T(8,128)S(1)} %broadcast_in_dim.19), channel_id=1, replica_groups=mesh['x'=4,'l'=4,'y'=4,'a'=2,'b'=2,'c'=2] {'x','y'}, dimensions={0} | all-to-all | bytes 131072 | tf_op jit(solution)/shard_map/all_to_all | solution.py:232
  15.4 0.7 broadcast_in_dim.20
  16.2 5.5 %all-to-all-start.2 = ((f32[4,16,8,128]{3,2,1,0:T(8,128)}), f32[4,16,8,128]{3,2,1,0:T(8,128)S(1)}, u32[]{:S(2)}, u32[]{:S(2)}) async-start(f32[4,16,8,128]{3,2,1,0:T(8,128)} %broadcast_in_dim.20), calls=%async_computation.2 | async-start | bytes 524288 | tf_op jit(solution)/shard_map/all_to_all | solution.py:232
  21.7 2.7 %copy.20 = bf16[1,2,143,2048]{3,2,1,0:T(8,128)(2,1)} copy(bf16[1,2,143,2048]{3,1,2,0:T(2,128)(2,1)} %param.7) | data formatting | bytes 2342912 | tf_op args[0]
  24.4 0.7 dynamic-slice_bitcast_fusion
  25.1 0.6 broadcast_in_dim.17.w_ref
  25.7 10.5 %channelize.1 = bf16[16,256,128]{2,1,0:T(8,128)(2,1)} custom-call(bf16[2,143,2048]{2,1,0:T(8,128)(2,1)} %bitcast.19, f32[16,2048]{1,0:T(8,128)} %constant.23.clone.h_ref, f32[2,16,128]{2,1,0:T(8,128)} %constant.24.clone.tw_ref, bf16[256,256]{1,0:T(8,128)(2,1)} %constant.25.clone.dhi_ref, bf16[256,256]{1,0:T(8,128)(2,1)} %constant.26.clone.dlo_ref, ...), custom_call_target="tpu_custom_call" | custom-call | tf_op jit(solution)/shard_map/channelize/pallas_call | solution.py:147
  36.2 3.4 %copy.14 = bf16[2,2,4,4,4,4,2,2,128]{8,7,2,1,4,0,6,5,3:T(2,128)(2,1)} copy(bf16[2,2,4,4,4,4,2,2,128]{8,7,6,5,4,3,2,1,0:T(2,128)(2,1)} %bitcast.20) | data formatting | bytes 2097152 | tf_op jit(solution)/shard_map/reshape | solution.py:244
  39.6 19.6 %all-to-all-start = ((bf16[512,8,128]{2,1,0:T(8,128)(2,1)}), bf16[512,8,128]{2,1,0:T(8,128)(2,1)S(1)}, u32[]{:S(2)}, u32[]{:S(2)}) async-start(bf16[512,8,128]{2,1,0:T(8,128)(2,1)} %bitcast.4), calls=%async_computation | async-start | bytes 2097152 | tf_op jit(solution)/shard_map/all_to_all | solution.py:246
  59.2 0.1 copy.18
  59.3 1.2 fusion.1
  60.5 0.2 copy.17
  60.7 0.1 mul.28
  60.8 0.1 iota_add_fusion
  60.9 0.1 add.31
  61.1 55.9 %all-to-all-done = bf16[512,8,128]{2,1,0:T(8,128)(2,1)S(1)} async-done(((bf16[512,8,128]{2,1,0:T(8,128)(2,1)}), bf16[512,8,128]{2,1,0:T(8,128)(2,1)S(1)}, u32[]{:S(2)}, u32[]{:S(2)}) %all-to-all-start) | async-done | bytes 1048608 | tf_op jit(solution)/shard_map/all_to_all | solution.py:246
  117.0 0.7 copy.15
  117.7 1.3 %copy.16 = bf16[512,4,256]{2,0,1:T(8,128)(2,1)} copy(bf16[512,4,256]{0,2,1:T(8,128)(2,1)S(1)} %bitcast.22) | data formatting | bytes 2097152 | tf_op jit(solution)/shard_map/reshape | solution.py:247
  119.0 0.6 broadcast_in_dim.21.row_ref
  119.6 0.8 broadcast_in_dim.45
  120.4 6.4 %correlate.1 = bf16[4,512,512]{2,1,0:T(8,128)(2,1)} custom-call(bf16[4,512,256]{2,1,0:T(8,128)(2,1)} %bitcast.21, s32[8,512]{1,0:T(8,128)} %broadcast_in_dim.21.row_ref, f32[512,128]{1,0:T(8,128)} %bitcast.25), custom_call_target="tpu_custom_call" | custom-call | tf_op jit(solution)/shard_map/correlate/pallas_call | solution.py:209
  (3 shorter events, 0.0 us)
Async XLA Ops:
  16.2 23.4 %all-to-all-start.2 = ((f32[4,16,8,128]{3,2,1,0:T(8,128)}), f32[4,16,8,128]{3,2,1,0:T(8,128)S(1)}, u32[]{:S(2)}, u32[]{:S(2)}) async-start(f32[4,16,8,128]{3,2,1,0:T(8,128)} %broadcast_in_dim.20), calls=%async_computation.2 | async-start | bytes 524288 | tf_op jit(solution)/shard_map/all_to_all | solution.py:232
  39.6 77.5 %all-to-all-start = ((bf16[512,8,128]{2,1,0:T(8,128)(2,1)}), bf16[512,8,128]{2,1,0:T(8,128)(2,1)S(1)}, u32[]{:S(2)}, u32[]{:S(2)}) async-start(bf16[512,8,128]{2,1,0:T(8,128)(2,1)} %bitcast.4), calls=%async_computation | async-start | bytes 2097152 | tf_op jit(solution)/shard_map/all_to_all | solution.py:246

commit v2 on v1

--- a/solution.py
+++ b/solution.py
@@ -73,22 +73,21 @@
     return out
 
 
-def channelize_kernel(v_ref, h_ref, tw_ref, dhi_ref, dlo_ref, w_ref, o_ref, xs_ref, f_ref, ahi_ref, alo_ref):
+def channelize_kernel(v_ref, h_ref, tw_ref, dhi_ref, dlo_ref, w_ref, z_ref, o_ref, xs_ref, f_ref, ahi_ref, alo_ref, m_ref):
     taps = h_ref.shape[0]
-    outer = xs_ref.shape[1]
-    spectra = o_ref.shape[2]
-    frames = v_ref.shape[1]
+    frames = v_ref.shape[0]
+    spectra = w_ref.shape[1]
 
     def filt(m, _):
         at = pl.multiple_of(m * 128, 128)
         for c in range(2):
-            xs_ref[c, 0, 0:frames, :] = v_ref[c, :, pl.ds(at, 128)].astype(F32)
+            xs_ref[c, 0:frames, :] = v_ref[:, c, pl.ds(at, 128)].astype(F32)
         rows = [h_ref[k : k + 1, pl.ds(at, 128)] for k in range(taps)]
         for c in range(2):
             for t in range(0, spectra, 8):
-                acc = rows[0] * xs_ref[c, 0, t : t + 8, :]
+                acc = rows[0] * xs_ref[c, t : t + 8, :]
                 for k in range(1, taps):
-                    acc = acc + rows[k] * xs_ref[c, 0, t + k : t + k + 8, :]
+                    acc = acc + rows[k] * xs_ref[c, t + k : t + k + 8, :]
                 f_ref[c, m, t : t + 8, :] = acc
         return 0
 
@@ -96,7 +95,6 @@
 
     def mix(tb, _):
         at = pl.multiple_of(tb * 16, 16)
-        parts = []
         for half in range(2):
             here = pl.multiple_of(at + 8 * half, 8)
             re = [f_ref[0, m, pl.ds(here, 8), :] for m in range(16)]
@@ -118,47 +116,52 @@
         return 0
 
     lax.fori_loop(0, spectra // 16, mix, 0)
-    weight = w_ref[0:1, :]
-
-    def turn(k, _):
+
+    def turn(q, _):
         def dot(a, b):
             return lax.dot_general(a, b, (((1,), (1,)), ((), ())), preferred_element_type=F32)
 
+        weight = w_ref[pl.ds(z_ref[0], 1), :]
         dhi, dlo = dhi_ref[...], dlo_ref[...]
-        hi, lo = ahi_ref[k], alo_ref[k]
-        out = dot(dhi, hi) + (dot(dhi, lo) + dot(dlo, hi))
-        out = out.astype(BF16).astype(F32) * weight
-        o_ref[k] = out.astype(BF16)
+        for i in range(4):
+            hi, lo = ahi_ref[4 * q + i], alo_ref[4 * q + i]
+            out = dot(dhi, hi) + (dot(dhi, lo) + dot(dlo, hi))
+            out = out.astype(BF16).astype(F32) * weight
+            for c in range(2):
+                m_ref[pl.ds(2 * i + c, 128, stride=8), :] = out[128 * c : 128 * (c + 1)]
+        o_ref[pl.ds(pl.multiple_of(q * 1024, 1024), 1024), :] = m_ref[...].astype(BF16)
         return 0
 
-    lax.fori_loop(0, 16, turn, 0)
-
-
-def channelize(voltages, weight_row, spectra, interpret=False):
-    _, frames, lanes = voltages.shape
+    lax.fori_loop(0, 4, turn, 0)
+
+
+def channelize(voltages, flags, station, spectra, interpret=False):
+    frames, _, lanes = voltages.shape
     taps = frames - spectra + 1
     h = filter_rows(taps, lanes)
     tw = twist_rows(16, 128)
     d = inner_matrix(128, 1.0 / math.sqrt(lanes))
-    dhi = jnp.asarray(d.astype(np.float32)).astype(BF16)
-    dhi_np = np.asarray(d.astype(np.float32)).astype(jnp.bfloat16)
-    dlo_np = (d - dhi_np.astype(np.float64)).astype(np.float32).astype(jnp.bfloat16)
-    padded = (frames + 15) // 16 * 16
+    d = d.reshape(4, 4, 4, 2, 2, 256).transpose(4, 0, 2, 3, 1, 5).reshape(256, 256)
+    dhi = d.astype(np.float32).astype(jnp.bfloat16)
+    dlo = (d - dhi.astype(np.float64)).astype(np.float32).astype(jnp.bfloat16)
+    padded = (frames + 7) // 8 * 8
     return pl.pallas_call(
         channelize_kernel,
-        out_shape=jax.ShapeDtypeStruct((16, 256, spectra), BF16),
+        out_shape=jax.ShapeDtypeStruct((4096, spectra), BF16),
         scratch_shapes=[
-            pltpu.VMEM((2, 1, padded, 128), F32),
+            pltpu.VMEM((2, padded, 128), F32),
             pltpu.VMEM((2, 16, spectra, 128), F32),
             pltpu.VMEM((16, spectra, 256), BF16),
             pltpu.VMEM((16, spectra, 256), BF16),
+            pltpu.VMEM((1024, spectra), F32),
         ],
+        in_specs=[pl.BlockSpec(memory_space=pltpu.VMEM)] * 6 + [pl.BlockSpec(memory_space=pltpu.SMEM)],
         interpret=interpret,
         name="channelize",
-    )(voltages, jnp.asarray(h), jnp.asarray(tw), jnp.asarray(dhi_np), jnp.asarray(dlo_np), weight_row)
-
-
-def correlate_kernel(x_ref, row_ref, flag_ref, o_ref, sel_ref, inv_ref):
+    )(voltages, jnp.asarray(h), jnp.asarray(tw), jnp.asarray(dhi), jnp.asarray(dlo), flags, station)
+
+
+def correlate_kernel(x_ref, row_ref, flag_ref, o_ref, sel_ref, inv_ref, s_ref):
     rows = sel_ref.shape[0]
 
     def nt(a, b):
@@ -182,8 +185,11 @@
         right = jnp.concatenate([hi, mid, hi, mid, low, hi], axis=1)
         count = nt(left, right)
         inv_ref[...] = 1.0 / jnp.maximum(count, 1.0)
-
-    kept = jnp.dot(sel_ref[...], x_ref[0], preferred_element_type=F32)
+        s_ref[...] = x_ref[...].astype(F32)
+
+    at = 2 * pl.program_id(0)
+    mine = jnp.concatenate([s_ref[pl.ds(at, rows, stride=8), :], s_ref[pl.ds(at + 1, rows, stride=8), :]], axis=1)
+    kept = jnp.dot(sel_ref[...], mine.astype(BF16), preferred_element_type=F32)
     half = kept.shape[1] // 2
     plain = kept.astype(BF16)
     turned = jnp.concatenate([-kept[:, half:], kept[:, :half]], axis=1).astype(BF16)
@@ -205,18 +211,22 @@
 
 
 def correlate(arrived, row_of, flags, interpret=False):
-    channels, inputs, wide = arrived.shape
+    channels, inputs = 4, flags.shape[0]
     return pl.pallas_call(
         correlate_kernel,
         grid=(channels,),
         in_specs=[
-            pl.BlockSpec((1, inputs, wide), lambda i: (i, 0, 0)),
+            pl.BlockSpec(arrived.shape, lambda i: (0, 0)),
             pl.BlockSpec(row_of.shape, lambda i: (0, 0)),
             pl.BlockSpec(flags.shape, lambda i: (0, 0)),
         ],
         out_specs=pl.BlockSpec((1, inputs, inputs), lambda i: (i, 0, 0)),
         out_shape=jax.ShapeDtypeStruct((channels, inputs, inputs), BF16),
-        scratch_shapes=[pltpu.VMEM((inputs, inputs), BF16), pltpu.VMEM((inputs, inputs), F32)],
+        scratch_shapes=[
+            pltpu.VMEM((inputs, inputs), BF16),
+            pltpu.VMEM((inputs, inputs), F32),
+            pltpu.VMEM(arrived.shape, F32),
+        ],
         interpret=interpret,
         name="correlate",
     )(arrived, row_of, flags)
@@ -224,32 +234,26 @@
 
 def gather_flags(flags, station_row):
     own = flags.shape[0]
-    tile = jnp.concatenate(
-        [flags, jnp.broadcast_to(station_row.astype(F32)[:, None], flags.shape)], axis=0
-    )
-    for axes, count in ((("x", "y"), 16), (("l",), 4)):
-        tile = jnp.broadcast_to(tile[None], (count,) + tile.shape)
-        tile = lax.all_to_all(tile, axes, split_axis=0, concat_axis=0, tiled=True)
-    tile = tile.reshape(4, 4, 4, 2, own, flags.shape[1])
-    return tile[..., 0, :, :], tile[..., 1, :, 0].astype(jnp.int32)
+    tile = jnp.concatenate([flags, jnp.broadcast_to(station_row.astype(F32)[:, None], flags.shape)], axis=0)
+    tile = jnp.broadcast_to(tile[None], (64,) + tile.shape)
+    tile = lax.all_to_all(tile, ("x", "l", "y"), split_axis=0, concat_axis=0, tiled=True)
+    return tile.reshape(4, 4, 4, 2, own, flags.shape[1])
 
 
 def on_device(voltages, flags, station_row):
     spectra = flags.shape[1]
     z_hi = 2 * lax.axis_index("a") + lax.axis_index("b")
-    flags_all, rows_all = gather_flags(flags, station_row)
-    weight = lax.dynamic_slice_in_dim(flags, z_hi, 1, 0)
-    weight = jnp.broadcast_to(weight, (8, spectra))
-    made = channelize(voltages[0], weight, spectra)
-    grid = made.reshape(2, 2, 4, 4, 4, 4, 2, 2, spectra)
-    blocks = jnp.transpose(grid, (3, 5, 6, 0, 4, 1, 2, 7, 8)).reshape(512, 8, spectra)
-    moved = lax.all_to_all(blocks, ("x", "y", "a", "b", "l", "c"), split_axis=0, concat_axis=0, tiled=True)
-    arrived = jnp.transpose(moved.reshape(512, 4, 2 * spectra), (1, 0, 2))
-    flag_src = jnp.transpose(flags_all, (1, 2, 3, 0, 4)).reshape(256, 1, spectra)
-    flag_src = jnp.broadcast_to(flag_src, (256, 2, spectra)).reshape(512, spectra)
-    row_src = 2 * jnp.transpose(rows_all, (1, 2, 3, 0)).reshape(256, 1) + jnp.arange(2, dtype=jnp.int32)[None]
-    row_src = jnp.broadcast_to(row_src.reshape(1, 512), (8, 512))
-    return correlate(arrived, row_src, flag_src)
+    tiles = gather_flags(flags, station_row)
+    blocks = channelize(
+        jnp.transpose(voltages[0], (1, 0, 2)), flags, z_hi.astype(jnp.int32).reshape(1), spectra
+    ).reshape(512, 8, spectra)
+    parts = tiles.reshape(4, 4, 4, 2, 2, 2, spectra).transpose(3, 5, 0, 2, 4, 1, 6)
+    flag_src = jnp.broadcast_to(parts[0].reshape(2, 1, 128, spectra), (2, 2, 128, spectra)).reshape(512, spectra)
+    row_src = parts[1, ..., 0].astype(jnp.int32).reshape(2, 1, 128)
+    row_src = (2 * row_src + jnp.arange(2, dtype=jnp.int32)[None, :, None]).reshape(1, 512)
+    blocks, flag_src, row_src = lax.optimization_barrier((blocks, flag_src, row_src))
+    moved = lax.all_to_all(blocks, ("b", "c", "x", "y", "a", "l"), split_axis=0, concat_axis=0, tiled=True)
+    return correlate(moved.reshape(4096, spectra), row_src, flag_src)
 
 
 def solution(mesh):

time: 127 us -> 127 us (level)
  blocking collectives: 13.9 us -> 77.4 us
  waiting for transfers between devices: 56 us -> 0.01 us
  starting transfers between devices: 25.2 us -> 12.5 us
  local copies, waits for them, and re-layouts: 12.1 us -> 15.7 us
    all_to_all x1, blocking collectives: 13.9 us -> 77.4 us  [on_device(): lax.all_to_all(blocks, ('b', 'c', 'x', 'y', 'a', 'l'), split_axis=0, conc...]
    all_to_all x2 -> x1, waiting for transfers between devices: 56 us -> 0.01 us  [gather_flags(): lax.all_to_all(tile, ('x', 'l', 'y'), split_axis=0, concat_axis=0, tiled=...]
    all_to_all x2 -> x1, starting transfers between devices: 25.2 us -> 12.5 us  [gather_flags(): lax.all_to_all(tile, ('x', 'l', 'y'), split_axis=0, concat_axis=0, tiled=...]
    slice x0 -> x2, local copies, waits for them, and re-layouts: none -> 8.17 us  [on_device(): parts[0].reshape(2, 1, 128, spectra)]
    another operation x0 -> x1, local copies, waits for them, and re-layouts: none -> 5.84 us  [on_device(): tiles.reshape(4, 4, 4, 2, 2, 2, spectra).transpose(3, 5, 0, 2, 4, 1, 6)]
    reshape x2 -> x0, local copies, waits for them, and re-layouts: 4.66 us -> none  [the longest x1 3.36 us: on_device(): grid = made.reshape(2, 2, 4, 4, 4, 4, 2, 2, spectra)]
    unnamed x1 -> x2, local copies, waits for them, and re-layouts: 2.7 us -> 0.01 us
    broadcast_in_dim x6 -> x2, local copies, waits for them, and re-layouts: 3.43 us -> 1.43 us  [the longest x1 0.72 us: on_device(): jnp.broadcast_to(parts[0].reshape(2, 1, 128, spectra), (2, 2, 128, spectra))]
  transfers between devices with their start and end apart: 2 -> 1, of which waited for: 1 -> 0; matrix products, arithmetic and copies ran while one was open for 7% -> 0% of each run, Pallas kernels for 8% -> 9%
where the time goes in v2:
time: 127 us
  blocking collectives  77.4 us (61%)
  Pallas kernels  18.2 us (14%)
  local copies, waits for them, and re-layouts  15.7 us (12%)
  starting transfers between devices  12.5 us (10%)
  other arithmetic  2.78 us (2%)
    all_to_all x1, blocking collectives, on_device(): lax.all_to_all(blocks, ('b', 'c', 'x', 'y', 'a', 'l'), split_axis=0, conc...  77.4 us
    all_to_all x1, starting transfers between devices, gather_flags(): lax.all_to_all(tile, ('x', 'l', 'y'), split_axis=0, concat_axis=0, tiled=...  12.5 us
    pallas_call x1, Pallas kernels, channelize(): pl.pallas_call(channelize_kernel, out_shape=jax.ShapeDtypeStruct((4096, s...  11.7 us
    slice x2, local copies, waits for them, and re-layouts, on_device(): parts[0].reshape(2, 1, 128, spectra)  8.17 us
    pallas_call x1, Pallas kernels, correlate(): pl.pallas_call(correlate_kernel, grid=(channels,), in_specs=[pl.BlockSpec...  6.43 us
    another operation x1, local copies, waits for them, and re-layouts, on_device(): tiles.reshape(4, 4, 4, 2, 2, 2, spectra).transpose(3, 5, 0, 2, 4, 1, 6)  5.84 us
  transfers between devices with their start and end apart: 1, of which 0 were waited for; matrix products, arithmetic and copies ran while one was open for 0% of the time, Pallas kernels for 9%

profile of v2, /device:TPU:1, one launch (start us, length us, event | category | flops | bytes accessed | tf_op | source)
XLA Modules:
  0.0 126.6 jit_solution(249360775362993344)
XLA Ops:
  0.0 0.7 convert_element_type.12
  0.7 0.1 pad.1.clone
  0.7 0.8 pad_maximum_fusion
  1.5 0.7 broadcast_in_dim.9
  2.2 12.5 %all-to-all-start = ((f32[64,8,128]{2,1,0:T(8,128)}), f32[64,8,128]{2,1,0:T(8,128)S(1)}, u32[]{:S(2)}, u32[]{:S(2)}) async-start(f32[64,8,128]{2,1,0:T(8,128)} %broadcast_in_dim.9), calls=%async_computation | async-start | bytes 524288 | tf_op jit(solution)/shard_map/all_to_all | solution.py:239
  14.7 11.7 %channelize.1 = bf16[4096,128]{1,0:T(8,128)(2,1)} custom-call(bf16[143,2,2048]{2,1,0:T(2,128)(2,1)} %bitcast.17, f32[16,2048]{1,0:T(8,128)} %constant.19.clone.h_ref, f32[2,16,128]{2,1,0:T(8,128)} %constant.20.clone.tw_ref, bf16[256,256]{1,0:T(8,128)(2,1)} %constant.21.clone.dhi_ref, bf16[256,256]{1,0:T(8,128)(2,1)} %constant.22.clone.dlo_ref, ...), custom_call_target="tpu_custom_call" | custom-call | tf_op jit(solution)/shard_map/channelize/pallas_call | solution.py:148
  26.5 0.0 all-to-all-done
  26.5 5.8 %copy.11 = f32[4,4,4,2,2,2,128]{1,2,6,4,0,5,3:T(4,128)} copy(f32[4,4,4,2,2,2,128]{6,5,4,3,2,1,0:T(2,128)S(1)} %bitcast.18) | data formatting | bytes 524288 | tf_op jit(solution)/shard_map/reshape;reshape | solution.py:250
  32.3 0.8 fusion
  33.1 4.5 %slice.8 = f32[1,2,4,4,2,4,128]{5,3,6,4,2,1,0:T(4,128)} slice(f32[2,2,4,4,2,4,128]{5,3,6,4,2,1,0:T(4,128)} %bitcast.14), slice={[0:1], [0:2], [0:4], [0:4], [0:2], [0:4], [0:128]} | slice | bytes 262144 | tf_op jit(solution)/shard_map/slice | solution.py:251
  37.6 0.0 copy-start
  37.6 3.6 %copy.12 = f32[1,2,4,4,2,4,128]{6,5,4,3,2,1,0:T(4,128)S(1)} copy(f32[1,2,4,4,2,4,128]{5,3,6,4,2,1,0:T(4,128)} %slice.8) | data formatting | bytes 262144 | tf_op jit(solution)/shard_map/slice | solution.py:251
  41.3 0.1 mul.20
  41.4 0.6 iota_add_fusion
  42.0 0.7 broadcast_in_dim.11
  42.7 0.0 copy-done
  42.7 77.4 %all_to_all.10 = bf16[512,8,128]{2,1,0:T(8,128)(2,1)} all-to-all(bf16[512,8,128]{2,1,0:T(8,128)(2,1)S(1)} %bitcast.16), channel_id=1, replica_groups=mesh['x'=4,'l'=4,'y'=4,'a'=2,'b'=2,'c'=2] {'b','c','x','y','a','l'}, dimensions={0} | all-to-all | bytes 2097152 | tf_op jit(solution)/shard_map/all_to_all | solution.py:255
  120.1 6.4 %correlate.1 = bf16[4,512,512]{2,1,0:T(8,128)(2,1)} custom-call(bf16[4096,128]{1,0:T(8,128)(2,1)} %bitcast.15, s32[1,512]{1,0:T(1,128)} %bitcast.21, f32[512,128]{1,0:T(8,128)} %bitcast.19), custom_call_target="tpu_custom_call" | custom-call | tf_op jit(solution)/shard_map/correlate/pallas_call | solution.py:215
  (1 shorter events, 0.0 us)
Async XLA Ops:
  2.2 24.3 %all-to-all-start = ((f32[64,8,128]{2,1,0:T(8,128)}), f32[64,8,128]{2,1,0:T(8,128)S(1)}, u32[]{:S(2)}, u32[]{:S(2)}) async-start(f32[64,8,128]{2,1,0:T(8,128)} %broadcast_in_dim.9), calls=%async_computation | async-start | bytes 524288 | tf_op jit(solution)/shard_map/all_to_all | solution.py:239
  37.6 5.1 %copy-start = (bf16[4096,128]{1,0:T(8,128)(2,1)S(1)}, bf16[4096,128]{1,0:T(8,128)(2,1)}, u32[]{:S(2)}) copy-start(bf16[4096,128]{1,0:T(8,128)(2,1)} %channelize.1) | copy-start | bytes 3145732

commit v3 on v2

--- a/solution.py
+++ b/solution.py
@@ -161,30 +161,51 @@
     )(voltages, jnp.asarray(h), jnp.asarray(tw), jnp.asarray(dhi), jnp.asarray(dlo), flags, station)
 
 
-def correlate_kernel(x_ref, row_ref, flag_ref, o_ref, sel_ref, inv_ref, s_ref):
+def nt(a, b):
+    return lax.dot_general(a, b, (((1,), (1,)), ((), ())), preferred_element_type=F32)
+
+
+def prepare_kernel(tile_ref, sel_ref, inv_ref):
     rows = sel_ref.shape[0]
-
-    def nt(a, b):
-        return lax.dot_general(a, b, (((1,), (1,)), ((), ())), preferred_element_type=F32)
+    tile = tile_ref[...]
+    n = tile.shape[1]
+    ids = jnp.transpose(tile)[0:8, :]
+    ids = jnp.concatenate([ids[:, 4:], ids[:, :4]], axis=1)
+    lane = lax.broadcasted_iota(jnp.int32, (8, rows), 1)
+    ids = jnp.where((lane & 7) < 4, ids, -1.0)
+    down = lax.broadcasted_iota(jnp.int32, (rows, rows), 0)
+    pol = (lane >> 7) & 1
+    spot = ((lane >> 3) & 15) * 32 + (lane & 3) * 8 + ((lane >> 2) & 1) * 2 + (lane >> 8)
+    move = jnp.where(down == spot[0:1], 1.0, 0.0).astype(BF16)
+    moved = jnp.dot(ids.astype(BF16), move, preferred_element_type=F32).astype(jnp.int32)
+    source_row = 2 * moved + pol
+    sel_ref[...] = jnp.where(down == source_row[0:1], 1.0, 0.0).astype(BF16)
+    pick = jnp.where((down >> 1) == ids[0:1].astype(jnp.int32), 1.0, 0.0).astype(BF16)
+    hi = tile.astype(BF16)
+    rest = tile - hi.astype(F32)
+    mid = rest.astype(BF16)
+    low = (rest - mid.astype(F32)).astype(BF16)
+    placed = jnp.dot(pick, jnp.concatenate([hi, mid, low], axis=1), preferred_element_type=F32).astype(BF16)
+    hi, mid, low = placed[:, :n], placed[:, n : 2 * n], placed[:, 2 * n :]
+    left = jnp.concatenate([hi, hi, mid, mid, hi, low], axis=1)
+    right = jnp.concatenate([hi, mid, hi, mid, low, hi], axis=1)
+    inv_ref[...] = 1.0 / jnp.maximum(nt(left, right), 1.0)
+
+
+def prepare(tile, inputs, interpret=False):
+    return pl.pallas_call(
+        prepare_kernel,
+        out_shape=(jax.ShapeDtypeStruct((inputs, inputs), BF16), jax.ShapeDtypeStruct((inputs, inputs), F32)),
+        interpret=interpret,
+        name="prepare",
+    )(tile)
+
+
+def correlate_kernel(x_ref, sel_ref, inv_ref, o_ref, s_ref):
+    rows = sel_ref.shape[0]
 
     @pl.when(pl.program_id(0) == 0)
     def _():
-        at = lax.broadcasted_iota(jnp.int32, (rows, rows), 0)
-        sel = jnp.where(row_ref[0:1, :] == at, 1.0, 0.0).astype(BF16)
-        sel_ref[...] = sel
-        flag = flag_ref[...]
-        hi = flag.astype(BF16)
-        rest = flag - hi.astype(F32)
-        mid = rest.astype(BF16)
-        low = (rest - mid.astype(F32)).astype(BF16)
-        pieces = jnp.concatenate([hi, mid, low], axis=1)
-        placed = jnp.dot(sel, pieces, preferred_element_type=F32).astype(BF16)
-        n = flag.shape[1]
-        hi, mid, low = placed[:, :n], placed[:, n : 2 * n], placed[:, 2 * n :]
-        left = jnp.concatenate([hi, hi, mid, mid, hi, low], axis=1)
-        right = jnp.concatenate([hi, mid, hi, mid, low, hi], axis=1)
-        count = nt(left, right)
-        inv_ref[...] = 1.0 / jnp.maximum(count, 1.0)
         s_ref[...] = x_ref[...].astype(F32)
 
     at = 2 * pl.program_id(0)
@@ -210,50 +231,31 @@
             o_ref[0, a * n : (a + 1) * n, b * n : (b + 1) * n] = (out * inv).astype(BF16)
 
 
-def correlate(arrived, row_of, flags, interpret=False):
-    channels, inputs = 4, flags.shape[0]
+def correlate(arrived, sel, inv, interpret=False):
+    inputs = sel.shape[0]
+    channels = arrived.shape[0] // (2 * inputs)
     return pl.pallas_call(
         correlate_kernel,
         grid=(channels,),
-        in_specs=[
-            pl.BlockSpec(arrived.shape, lambda i: (0, 0)),
-            pl.BlockSpec(row_of.shape, lambda i: (0, 0)),
-            pl.BlockSpec(flags.shape, lambda i: (0, 0)),
-        ],
+        in_specs=[pl.BlockSpec(x.shape, lambda i: (0, 0)) for x in (arrived, sel, inv)],
         out_specs=pl.BlockSpec((1, inputs, inputs), lambda i: (i, 0, 0)),
         out_shape=jax.ShapeDtypeStruct((channels, inputs, inputs), BF16),
-        scratch_shapes=[
-            pltpu.VMEM((inputs, inputs), BF16),
-            pltpu.VMEM((inputs, inputs), F32),
-            pltpu.VMEM(arrived.shape, F32),
-        ],
+        scratch_shapes=[pltpu.VMEM(arrived.shape, F32)],
         interpret=interpret,
         name="correlate",
-    )(arrived, row_of, flags)
-
-
-def gather_flags(flags, station_row):
-    own = flags.shape[0]
+    )(arrived, sel, inv)
+
+
+def on_device(voltages, flags, station_row):
+    spectra = flags.shape[1]
+    z_hi = (2 * lax.axis_index("a") + lax.axis_index("b")).astype(jnp.int32).reshape(1)
     tile = jnp.concatenate([flags, jnp.broadcast_to(station_row.astype(F32)[:, None], flags.shape)], axis=0)
     tile = jnp.broadcast_to(tile[None], (64,) + tile.shape)
-    tile = lax.all_to_all(tile, ("x", "l", "y"), split_axis=0, concat_axis=0, tiled=True)
-    return tile.reshape(4, 4, 4, 2, own, flags.shape[1])
-
-
-def on_device(voltages, flags, station_row):
-    spectra = flags.shape[1]
-    z_hi = 2 * lax.axis_index("a") + lax.axis_index("b")
-    tiles = gather_flags(flags, station_row)
-    blocks = channelize(
-        jnp.transpose(voltages[0], (1, 0, 2)), flags, z_hi.astype(jnp.int32).reshape(1), spectra
-    ).reshape(512, 8, spectra)
-    parts = tiles.reshape(4, 4, 4, 2, 2, 2, spectra).transpose(3, 5, 0, 2, 4, 1, 6)
-    flag_src = jnp.broadcast_to(parts[0].reshape(2, 1, 128, spectra), (2, 2, 128, spectra)).reshape(512, spectra)
-    row_src = parts[1, ..., 0].astype(jnp.int32).reshape(2, 1, 128)
-    row_src = (2 * row_src + jnp.arange(2, dtype=jnp.int32)[None, :, None]).reshape(1, 512)
-    blocks, flag_src, row_src = lax.optimization_barrier((blocks, flag_src, row_src))
+    tile = lax.all_to_all(tile, ("x", "y", "l"), split_axis=0, concat_axis=0, tiled=True)
+    blocks = channelize(jnp.transpose(voltages[0], (1, 0, 2)), flags, z_hi, spectra).reshape(512, 8, spectra)
     moved = lax.all_to_all(blocks, ("b", "c", "x", "y", "a", "l"), split_axis=0, concat_axis=0, tiled=True)
-    return correlate(moved.reshape(4096, spectra), row_src, flag_src)
+    sel, inv = prepare(tile.reshape(512, spectra), 512)
+    return correlate(moved.reshape(4096, spectra), sel, inv)
 
 
 def solution(mesh):

time: 127 us -> 111 us (0.87)
  blocking collectives: 77.4 us -> 0 us
  waiting for transfers between devices: 0.01 us -> 53.1 us
  starting transfers between devices: 12.5 us -> 33.6 us
  local copies, waits for them, and re-layouts: 15.7 us -> 1.84 us
  Pallas kernels: 18.2 us -> 21 us
  other arithmetic: 2.78 us -> 1.41 us
    all_to_all x1 -> x0, blocking collectives: 77.4 us -> none  [on_device(): lax.all_to_all(blocks, ('b', 'c', 'x', 'y', 'a', 'l'), split_axis=0, conc...]
    all_to_all x1 -> x2, waiting for transfers between devices: 0.01 us -> 53.1 us  [the longest x1 53 us: on_device(): lax.all_to_all(blocks, ('b', 'c', 'x', 'y', 'a', 'l'), split_axis=0, conc...]
    all_to_all x1 -> x2, starting transfers between devices: 12.5 us -> 33.6 us  [the longest x1 21.1 us: on_device(): lax.all_to_all(blocks, ('b', 'c', 'x', 'y', 'a', 'l'), split_axis=0, conc...]
    slice x2 -> x0, local copies, waits for them, and re-layouts: 8.17 us -> none  [on_device(): parts[0].reshape(2, 1, 128, spectra)]
    another operation x1 -> x0, local copies, waits for them, and re-layouts: 5.84 us -> none  [on_device(): tiles.reshape(4, 4, 4, 2, 2, 2, spectra).transpose(3, 5, 0, 2, 4, 1, 6)]
    pallas_call x0 -> x1, Pallas kernels: none -> 3.38 us  [prepare(): pl.pallas_call(prepare_kernel, out_shape=(jax.ShapeDtypeStruct((inputs, i...]
  transfers between devices with their start and end apart: 1 -> 2, of which waited for: 0 -> 1; matrix products, arithmetic and copies ran while one was open for 0% -> 0% of each run, Pallas kernels for 9% -> 14%
where the time goes in v3:
time: 111 us
  waiting for transfers between devices  53.1 us (48%)
  starting transfers between devices  33.6 us (30%)
  Pallas kernels  21 us (19%)
  local copies, waits for them, and re-layouts  1.84 us (2%)
  other arithmetic  1.41 us (1%)
    all_to_all x1, waiting for transfers between devices, on_device(): lax.all_to_all(blocks, ('b', 'c', 'x', 'y', 'a', 'l'), split_axis=0, conc...  53 us
    all_to_all x1, starting transfers between devices, on_device(): lax.all_to_all(blocks, ('b', 'c', 'x', 'y', 'a', 'l'), split_axis=0, conc...  21.1 us
    all_to_all x1, starting transfers between devices, on_device(): lax.all_to_all(tile, ('x', 'y', 'l'), split_axis=0, concat_axis=0, tiled=...  12.5 us
    pallas_call x1, Pallas kernels, channelize(): pl.pallas_call(channelize_kernel, out_shape=jax.ShapeDtypeStruct((4096, s...  11.7 us
    pallas_call x1, Pallas kernels, correlate(): pl.pallas_call(correlate_kernel, grid=(channels,), in_specs=[pl.BlockSpec...  5.92 us
    pallas_call x1, Pallas kernels, prepare(): pl.pallas_call(prepare_kernel, out_shape=(jax.ShapeDtypeStruct((inputs, i...  3.38 us
  transfers between devices with their start and end apart: 2, of which 1 were waited for; matrix products, arithmetic and copies ran while one was open for 0% of the time, Pallas kernels for 14%

profile of v3, /device:TPU:1, one launch (start us, length us, event | category | flops | bytes accessed | tf_op | source)
XLA Modules:
  0.0 111.0 jit_solution(10576964957736234319)
XLA Ops:
  0.0 0.7 convert_element_type.3
  0.7 0.1 pad.1.clone
  0.7 0.8 pad_maximum_fusion
  1.5 0.7 broadcast_in_dim.5
  2.2 12.5 %all-to-all-start.1 = ((f32[64,8,128]{2,1,0:T(8,128)}), f32[64,8,128]{2,1,0:T(8,128)S(1)}, u32[]{:S(2)}, u32[]{:S(2)}) async-start(f32[64,8,128]{2,1,0:T(8,128)} %broadcast_in_dim.5), calls=%async_computation.1 | async-start | bytes 524288 | tf_op jit(solution)/shard_map/all_to_all | solution.py:254
  14.8 11.7 %channelize.1 = bf16[4096,128]{1,0:T(8,128)(2,1)} custom-call(bf16[143,2,2048]{2,1,0:T(2,128)(2,1)} %bitcast.9, f32[16,2048]{1,0:T(8,128)} %constant.18.clone.h_ref, f32[2,16,128]{2,1,0:T(8,128)} %constant.19.clone.tw_ref, bf16[256,256]{1,0:T(8,128)(2,1)} %constant.20.clone.dhi_ref, bf16[256,256]{1,0:T(8,128)(2,1)} %constant.21.clone.dlo_ref, ...), custom_call_target="tpu_custom_call" | custom-call | tf_op jit(solution)/shard_map/channelize/pallas_call | solution.py:148
  26.5 0.0 all-to-all-done.1
  26.5 0.0 copy-start.1
  26.5 21.1 %all-to-all-start = ((bf16[512,8,128]{2,1,0:T(8,128)(2,1)}), bf16[512,8,128]{2,1,0:T(8,128)(2,1)S(1)}, u32[]{:S(2)}, u32[]{:S(2)}) async-start(bf16[512,8,128]{2,1,0:T(8,128)(2,1)} %bitcast.7), calls=%async_computation | async-start | bytes 2097152 | tf_op jit(solution)/shard_map/all_to_all | solution.py:256
  47.6 0.0 copy-done.1
  47.6 3.4 %prepare.1 = (bf16[512,512]{1,0:T(8,128)(2,1)}, f32[512,512]{1,0:T(8,128)}) custom-call(f32[512,128]{1,0:T(8,128)} %bitcast.10), custom_call_target="tpu_custom_call" | custom-call | tf_op jit(solution)/shard_map/prepare/pallas_call | solution.py:196
  50.9 53.0 %all-to-all-done = bf16[512,8,128]{2,1,0:T(8,128)(2,1)S(1)} async-done(((bf16[512,8,128]{2,1,0:T(8,128)(2,1)}), bf16[512,8,128]{2,1,0:T(8,128)(2,1)S(1)}, u32[]{:S(2)}, u32[]{:S(2)}) %all-to-all-start) | async-done | bytes 1048608 | tf_op jit(solution)/shard_map/all_to_all | solution.py:256
  104.0 0.0 copy-start
  104.0 1.0 copy-done
  105.0 5.9 %correlate.1 = bf16[4,512,512]{2,1,0:T(8,128)(2,1)} custom-call(bf16[4096,128]{1,0:T(8,128)(2,1)} %bitcast.8, bf16[512,512]{1,0:T(8,128)(2,1)} %get-tuple-element.7.sel_ref, f32[512,512]{1,0:T(8,128)} %get-tuple-element.8.inv_ref), custom_call_target="tpu_custom_call" | custom-call | tf_op jit(solution)/shard_map/correlate/pallas_call | solution.py:237
Async XLA Ops:
  2.2 24.3 %all-to-all-start.1 = ((f32[64,8,128]{2,1,0:T(8,128)}), f32[64,8,128]{2,1,0:T(8,128)S(1)}, u32[]{:S(2)}, u32[]{:S(2)}) async-start(f32[64,8,128]{2,1,0:T(8,128)} %broadcast_in_dim.5), calls=%async_computation.1 | async-start | bytes 524288 | tf_op jit(solution)/shard_map/all_to_all | solution.py:254
  26.5 21.1 %copy-start.1 = (f32[64,8,128]{2,1,0:T(8,128)}, f32[64,8,128]{2,1,0:T(8,128)S(1)}, u32[]{:S(2)}) copy-start(f32[64,8,128]{2,1,0:T(8,128)S(1)} %all-to-all-done.1) | copy-start | bytes 786436
  26.5 77.5 %all-to-all-start = ((bf16[512,8,128]{2,1,0:T(8,128)(2,1)}), bf16[512,8,128]{2,1,0:T(8,128)(2,1)S(1)}, u32[]{:S(2)}, u32[]{:S(2)}) async-start(bf16[512,8,128]{2,1,0:T(8,128)(2,1)} %bitcast.7), calls=%async_computation | async-start | bytes 2097152 | tf_op jit(solution)/shard_map/all_to_all | solution.py:256
  104.0 1.0 copy-start

commit v4 on v3

--- a/solution.py
+++ b/solution.py
@@ -73,43 +73,51 @@
     return out
 
 
-def channelize_kernel(v_ref, h_ref, tw_ref, dhi_ref, dlo_ref, w_ref, z_ref, o_ref, xs_ref, f_ref, ahi_ref, alo_ref, m_ref):
-    taps = h_ref.shape[0]
-    frames = v_ref.shape[0]
+def channelize_kernel(v_ref, h_ref, tw_ref, dhi_ref, dlo_ref, w_ref, z_ref, o_ref, x_ref, f_ref, g_ref, ahi_ref, alo_ref, m_ref):
+    taps = h_ref.shape[0] // 32
     spectra = w_ref.shape[1]
 
-    def filt(m, _):
-        at = pl.multiple_of(m * 128, 128)
-        for c in range(2):
-            xs_ref[c, 0:frames, :] = v_ref[:, c, pl.ds(at, 128)].astype(F32)
-        rows = [h_ref[k : k + 1, pl.ds(at, 128)] for k in range(taps)]
-        for c in range(2):
-            for t in range(0, spectra, 8):
-                acc = rows[0] * xs_ref[c, t : t + 8, :]
+    def widen(f, _):
+        at = pl.multiple_of(f * 352, 352)
+        x_ref[pl.ds(at, 352), :] = v_ref[pl.ds(at, 352), :].astype(F32)
+        return 0
+
+    lax.fori_loop(0, x_ref.shape[0] // 352, widen, 0)
+    pitch = f_ref.shape[0] // spectra
+    step = 16
+
+    for g in range(0, 32, 8):
+
+        def filt(tb, _):
+            first = tb * step
+            rows = [h_ref[32 * k + g : 32 * k + g + 8, :] for k in range(taps)]
+            x = [x_ref[pl.ds(pl.multiple_of((first + t) * 32 + g, 8), 8), :] for t in range(step + taps - 1)]
+            for t in range(step):
+                acc = rows[0] * x[t]
                 for k in range(1, taps):
-                    acc = acc + rows[k] * xs_ref[c, t + k : t + k + 8, :]
-                f_ref[c, m, t : t + 8, :] = acc
-        return 0
-
-    lax.fori_loop(0, f_ref.shape[1], filt, 0)
+                    acc = acc + rows[k] * x[t + k]
+                f_ref[pl.ds((first + t) * pitch + g, 8), :] = acc
+            return 0
+
+        lax.fori_loop(0, spectra // step, filt, 0)
 
     def mix(tb, _):
         at = pl.multiple_of(tb * 16, 16)
         for half in range(2):
             here = pl.multiple_of(at + 8 * half, 8)
-            re = [f_ref[0, m, pl.ds(here, 8), :] for m in range(16)]
-            im = [f_ref[1, m, pl.ds(here, 8), :] for m in range(16)]
+            re = [f_ref[pl.ds(here * pitch + 2 * m, 8, stride=pitch), :] for m in range(16)]
+            im = [f_ref[pl.ds(here * pitch + 2 * m + 1, 8, stride=pitch), :] for m in range(16)]
             out = small_transform(re, im)
             for k in range(16):
                 r, i = out[k]
                 if k:
                     cos, sin = tw_ref[0, k : k + 1, :], tw_ref[1, k : k + 1, :]
                     r, i = r * cos + i * sin, i * cos - r * sin
-                f_ref[0, k, pl.ds(here, 8), :] = r
-                f_ref[1, k, pl.ds(here, 8), :] = i
+                g_ref[0, k, pl.ds(here, 8), :] = r
+                g_ref[1, k, pl.ds(here, 8), :] = i
         for k in range(16):
             for c in range(2):
-                val = f_ref[c, k, pl.ds(at, 16), :]
+                val = g_ref[c, k, pl.ds(at, 16), :]
                 hi = val.astype(BF16)
                 ahi_ref[k, pl.ds(at, 16), c * 128 : (c + 1) * 128] = hi
                 alo_ref[k, pl.ds(at, 16), c * 128 : (c + 1) * 128] = (val - hi.astype(F32)).astype(BF16)
@@ -136,20 +144,22 @@
 
 
 def channelize(voltages, flags, station, spectra, interpret=False):
-    frames, _, lanes = voltages.shape
+    lanes = 2048
+    frames = voltages.shape[0] // 32
     taps = frames - spectra + 1
-    h = filter_rows(taps, lanes)
+    h = np.repeat(filter_rows(taps, lanes).reshape(taps * 16, 128), 2, axis=0)
     tw = twist_rows(16, 128)
     d = inner_matrix(128, 1.0 / math.sqrt(lanes))
     d = d.reshape(4, 4, 4, 2, 2, 256).transpose(4, 0, 2, 3, 1, 5).reshape(256, 256)
     dhi = d.astype(np.float32).astype(jnp.bfloat16)
     dlo = (d - dhi.astype(np.float64)).astype(np.float32).astype(jnp.bfloat16)
-    padded = (frames + 7) // 8 * 8
+    tables = [jnp.asarray(x) for x in (h, tw, dhi, dlo)]
     return pl.pallas_call(
         channelize_kernel,
         out_shape=jax.ShapeDtypeStruct((4096, spectra), BF16),
         scratch_shapes=[
-            pltpu.VMEM((2, padded, 128), F32),
+            pltpu.VMEM(voltages.shape, F32),
+            pltpu.VMEM((spectra * 36, 128), F32),
             pltpu.VMEM((2, 16, spectra, 128), F32),
             pltpu.VMEM((16, spectra, 256), BF16),
             pltpu.VMEM((16, spectra, 256), BF16),
@@ -158,7 +168,7 @@
         in_specs=[pl.BlockSpec(memory_space=pltpu.VMEM)] * 6 + [pl.BlockSpec(memory_space=pltpu.SMEM)],
         interpret=interpret,
         name="channelize",
-    )(voltages, jnp.asarray(h), jnp.asarray(tw), jnp.asarray(dhi), jnp.asarray(dlo), flags, station)
+    )(voltages, *tables, flags, station)
 
 
 def nt(a, b):
@@ -197,6 +207,7 @@
         prepare_kernel,
         out_shape=(jax.ShapeDtypeStruct((inputs, inputs), BF16), jax.ShapeDtypeStruct((inputs, inputs), F32)),
         interpret=interpret,
+        compiler_params=pltpu.CompilerParams(vmem_limit_bytes=24 << 20),
         name="prepare",
     )(tile)
 
@@ -208,51 +219,75 @@
     def _():
         s_ref[...] = x_ref[...].astype(F32)
 
-    at = 2 * pl.program_id(0)
-    mine = jnp.concatenate([s_ref[pl.ds(at, rows, stride=8), :], s_ref[pl.ds(at + 1, rows, stride=8), :]], axis=1)
-    kept = jnp.dot(sel_ref[...], mine.astype(BF16), preferred_element_type=F32)
-    half = kept.shape[1] // 2
-    plain = kept.astype(BF16)
-    turned = jnp.concatenate([-kept[:, half:], kept[:, :half]], axis=1).astype(BF16)
     n = rows // 2
-    for a in range(2):
-        for b in range(2):
-            pa = plain[a * n : (a + 1) * n]
-            if a > b:
-                out = nt(pa, plain[b * n : (b + 1) * n])
-            elif a < b:
-                out = nt(pa, turned[b * n : (b + 1) * n])
-            else:
-                real = nt(pa, pa)
-                imag = nt(pa, turned[b * n : (b + 1) * n])
-                below = lax.broadcasted_iota(jnp.int32, (n, n), 0) >= lax.broadcasted_iota(jnp.int32, (n, n), 1)
-                out = jnp.where(below, real, imag)
-            inv = inv_ref[a * n : (a + 1) * n, b * n : (b + 1) * n]
-            o_ref[0, a * n : (a + 1) * n, b * n : (b + 1) * n] = (out * inv).astype(BF16)
+    half = x_ref.shape[1]
+    below = lax.broadcasted_iota(jnp.int32, (n, n), 0) >= lax.broadcasted_iota(jnp.int32, (n, n), 1)
+    ready = []
+    for u in range(o_ref.shape[0]):
+        at = 2 * (pl.program_id(0) * o_ref.shape[0] + u)
+        mine = jnp.concatenate([s_ref[pl.ds(at, rows, stride=8), :], s_ref[pl.ds(at + 1, rows, stride=8), :]], axis=1)
+        kept = jnp.dot(sel_ref[...], mine.astype(BF16), preferred_element_type=F32)
+        turned = jnp.concatenate([-kept[:, half:], kept[:, :half]], axis=1).astype(BF16)
+        ready.append((kept.astype(BF16), turned))
+    for u, (plain, turned) in enumerate(ready):
+        for a in range(2):
+            for b in range(2):
+                pa = plain[a * n : (a + 1) * n]
+                if a > b:
+                    out = nt(pa, plain[b * n : (b + 1) * n])
+                elif a < b:
+                    out = nt(pa, turned[b * n : (b + 1) * n])
+                else:
+                    out = jnp.where(below, nt(pa, pa), nt(pa, turned[b * n : (b + 1) * n]))
+                inv = inv_ref[a * n : (a + 1) * n, b * n : (b + 1) * n]
+                o_ref[u, a * n : (a + 1) * n, b * n : (b + 1) * n] = (out * inv).astype(BF16)
 
 
 def correlate(arrived, sel, inv, interpret=False):
     inputs = sel.shape[0]
     channels = arrived.shape[0] // (2 * inputs)
+    arrived, sel, inv = (pltpu.with_memory_space_constraint(x, pltpu.VMEM) for x in (arrived, sel, inv))
     return pl.pallas_call(
         correlate_kernel,
-        grid=(channels,),
-        in_specs=[pl.BlockSpec(x.shape, lambda i: (0, 0)) for x in (arrived, sel, inv)],
-        out_specs=pl.BlockSpec((1, inputs, inputs), lambda i: (i, 0, 0)),
+        grid=(channels // 2,),
+        in_specs=[pl.BlockSpec(memory_space=pltpu.VMEM)] * 3,
+        out_specs=pl.BlockSpec((2, inputs, inputs), lambda i: (i, 0, 0)),
         out_shape=jax.ShapeDtypeStruct((channels, inputs, inputs), BF16),
         scratch_shapes=[pltpu.VMEM(arrived.shape, F32)],
         interpret=interpret,
+        compiler_params=pltpu.CompilerParams(vmem_limit_bytes=24 << 20),
         name="correlate",
     )(arrived, sel, inv)
+
+
+def tile_kernel(flag_ref, row_ref, o_ref):
+    own, n = flag_ref.shape
+    down = lax.broadcasted_iota(jnp.int32, (own, n), 0)
+    ids = jnp.zeros((own, n), jnp.int32)
+    for q in range(own):
+        ids = jnp.where(down == q, row_ref[q], ids)
+    block = jnp.concatenate([flag_ref[...], ids.astype(F32)], axis=0)
+    for d in range(o_ref.shape[0]):
+        o_ref[d] = block
+
+
+def make_tiles(flags, station_row, copies, interpret=False):
+    return pl.pallas_call(
+        tile_kernel,
+        out_shape=jax.ShapeDtypeStruct((copies, 2 * flags.shape[0], flags.shape[1]), F32),
+        in_specs=[pl.BlockSpec(memory_space=pltpu.VMEM), pl.BlockSpec(memory_space=pltpu.SMEM)],
+        interpret=interpret,
+        name="make_tiles",
+    )(flags, station_row)
 
 
 def on_device(voltages, flags, station_row):
     spectra = flags.shape[1]
     z_hi = (2 * lax.axis_index("a") + lax.axis_index("b")).astype(jnp.int32).reshape(1)
-    tile = jnp.concatenate([flags, jnp.broadcast_to(station_row.astype(F32)[:, None], flags.shape)], axis=0)
-    tile = jnp.broadcast_to(tile[None], (64,) + tile.shape)
+    tile = make_tiles(flags, station_row, 64)
     tile = lax.all_to_all(tile, ("x", "y", "l"), split_axis=0, concat_axis=0, tiled=True)
-    blocks = channelize(jnp.transpose(voltages[0], (1, 0, 2)), flags, z_hi, spectra).reshape(512, 8, spectra)
+    frames = jnp.transpose(voltages[0].reshape(2, -1, 16, 128), (1, 2, 0, 3)).reshape(-1, 128)
+    blocks = channelize(frames, flags, z_hi, spectra).reshape(512, 8, spectra)
     moved = lax.all_to_all(blocks, ("b", "c", "x", "y", "a", "l"), split_axis=0, concat_axis=0, tiled=True)
     sel, inv = prepare(tile.reshape(512, spectra), 512)
     return correlate(moved.reshape(4096, spectra), sel, inv)

time: 111 us -> 104 us (0.937)
  Pallas kernels: 21 us -> 14.5 us
  waiting for transfers between devices: 53.1 us -> 57.6 us
  starting transfers between devices: 33.6 us -> 31.5 us
  local copies, waits for them, and re-layouts: 1.84 us -> 0 us
  other arithmetic: 1.41 us -> 0 us
    pallas_call x1, Pallas kernels: 11.7 us -> 8.48 us  [channelize(): pl.pallas_call(channelize_kernel, out_shape=jax.ShapeDtypeStruct((4096, s...]
    all_to_all x1, waiting for transfers between devices: 0.01 us -> 2.57 us  [on_device(): lax.all_to_all(tile, ('x', 'y', 'l'), split_axis=0, concat_axis=0, tiled=...]
    all_to_all x1, starting transfers between devices: 21.1 us -> 19 us  [on_device(): lax.all_to_all(blocks, ('b', 'c', 'x', 'y', 'a', 'l'), split_axis=0, conc...]
    all_to_all x1, waiting for transfers between devices: 53 us -> 55 us  [on_device(): lax.all_to_all(blocks, ('b', 'c', 'x', 'y', 'a', 'l'), split_axis=0, conc...]
    pallas_call x1, Pallas kernels: 3.38 us -> 1.43 us  [prepare(): pl.pallas_call(prepare_kernel, out_shape=(jax.ShapeDtypeStruct((inputs, i...]
    pallas_call x1 -> x2, Pallas kernels: 5.92 us -> 4.59 us  [the longest x1 3.08 us: correlate(): pl.pallas_call(correlate_kernel, grid=(channels // 2,), in_specs=[pl.Bloc...]
  transfers between devices with their start and end apart: 2 -> 2, of which waited for: 1 -> 2; matrix products, arithmetic and copies ran while one was open for 0% -> 0% of each run, Pallas kernels for 14% -> 10%
where the time goes in v4:
time: 104 us
  waiting for transfers between devices  57.6 us (55%)
  starting transfers between devices  31.5 us (30%)
  Pallas kernels  14.5 us (14%)
    all_to_all x1, waiting for transfers between devices, on_device(): lax.all_to_all(blocks, ('b', 'c', 'x', 'y', 'a', 'l'), split_axis=0, conc...  55 us
    all_to_all x1, starting transfers between devices, on_device(): lax.all_to_all(blocks, ('b', 'c', 'x', 'y', 'a', 'l'), split_axis=0, conc...  19 us
    all_to_all x1, starting transfers between devices, on_device(): lax.all_to_all(tile, ('x', 'y', 'l'), split_axis=0, concat_axis=0, tiled=...  12.5 us
    pallas_call x1, Pallas kernels, channelize(): pl.pallas_call(channelize_kernel, out_shape=jax.ShapeDtypeStruct((4096, s...  8.48 us
    pallas_call x1, Pallas kernels, correlate(): pl.pallas_call(correlate_kernel, grid=(channels // 2,), in_specs=[pl.Bloc...  3.08 us
    all_to_all x1, waiting for transfers between devices, on_device(): lax.all_to_all(tile, ('x', 'y', 'l'), split_axis=0, concat_axis=0, tiled=...  2.57 us
  transfers between devices with their start and end apart: 2, of which 2 were waited for; matrix products, arithmetic and copies ran while one was open for 0% of the time, Pallas kernels for 10%

profile of v4, /device:TPU:1, one launch (start us, length us, event | category | flops | bytes accessed | tf_op | source)
XLA Modules:
  0.0 103.6 jit_solution(13982157309371488630)
XLA Ops:
  0.0 1.5 %make_tiles.1 = f32[64,8,128]{2,1,0:T(8,128)} custom-call(f32[4,128]{1,0:T(4,128)} %flag_ref.1, s32[4]{0:T(128)} %row_ref.1), custom_call_target="tpu_custom_call" | custom-call | tf_op jit(solution)/shard_map/make_tiles/pallas_call | solution.py:275
  1.5 12.5 %all-to-all-start.1 = ((f32[64,8,128]{2,1,0:T(8,128)}), f32[64,8,128]{2,1,0:T(8,128)S(1)}, u32[]{:S(2)}, u32[]{:S(2)}) async-start(f32[64,8,128]{2,1,0:T(8,128)} %make_tiles.1), calls=%async_computation.1 | async-start | bytes 524288 | tf_op jit(solution)/shard_map/all_to_all | solution.py:288
  14.1 8.5 %channelize.1 = bf16[4096,128]{1,0:T(8,128)(2,1)} custom-call(bf16[4576,128]{1,0:T(8,128)(2,1)} %bitcast.12, f32[512,128]{1,0:T(8,128)} %constant.18.clone.h_ref, f32[2,16,128]{2,1,0:T(8,128)} %constant.19.clone.tw_ref, bf16[256,256]{1,0:T(8,128)(2,1)} %constant.20.clone.dhi_ref, bf16[256,256]{1,0:T(8,128)(2,1)} %constant.21.clone.dlo_ref, ...), custom_call_target="tpu_custom_call" | custom-call | tf_op jit(solution)/shard_map/channelize/pallas_call | solution.py:157
  22.5 2.6 %all-to-all-done.1 = f32[64,8,128]{2,1,0:T(8,128)S(1)} async-done(((f32[64,8,128]{2,1,0:T(8,128)}), f32[64,8,128]{2,1,0:T(8,128)S(1)}, u32[]{:S(2)}, u32[]{:S(2)}) %all-to-all-start.1) | async-done | bytes 262176 | tf_op jit(solution)/shard_map/all_to_all | solution.py:288
  25.1 19.0 %all-to-all-start = ((bf16[512,8,128]{2,1,0:T(8,128)(2,1)}), bf16[512,8,128]{2,1,0:T(8,128)(2,1)S(1)}, u32[]{:S(2)}, u32[]{:S(2)}) async-start(bf16[512,8,128]{2,1,0:T(8,128)(2,1)} %bitcast.11), calls=%async_computation | async-start | bytes 2097152 | tf_op jit(solution)/shard_map/all_to_all | solution.py:291
  44.1 1.4 %prepare.1 = (bf16[512,512]{1,0:T(8,128)(2,1)S(1)}, f32[512,512]{1,0:T(8,128)S(1)}) custom-call(f32[512,128]{1,0:T(8,128)S(1)} %bitcast.10), custom_call_target="tpu_custom_call" | custom-call | tf_op jit(solution)/shard_map/prepare/pallas_call | solution.py:206
  45.5 55.0 %all-to-all-done = bf16[512,8,128]{2,1,0:T(8,128)(2,1)S(1)} async-done(((bf16[512,8,128]{2,1,0:T(8,128)(2,1)}), bf16[512,8,128]{2,1,0:T(8,128)(2,1)S(1)}, u32[]{:S(2)}, u32[]{:S(2)}) %all-to-all-start) | async-done | bytes 1048608 | tf_op jit(solution)/shard_map/all_to_all | solution.py:291
  100.5 3.1 %correlate.1 = bf16[4,512,512]{2,1,0:T(8,128)(2,1)} custom-call(bf16[4096,128]{1,0:T(8,128)(2,1)S(1)} %bitcast.9, bf16[512,512]{1,0:T(8,128)(2,1)S(1)} %get-tuple-element.7.sel_ref, f32[512,512]{1,0:T(8,128)S(1)} %get-tuple-element.8.inv_ref), custom_call_target="tpu_custom_call" | custom-call | tf_op jit(solution)/shard_map/correlate/pallas_call | solution.py:250
Async XLA Ops:
  1.5 23.6 %all-to-all-start.1 = ((f32[64,8,128]{2,1,0:T(8,128)}), f32[64,8,128]{2,1,0:T(8,128)S(1)}, u32[]{:S(2)}, u32[]{:S(2)}) async-start(f32[64,8,128]{2,1,0:T(8,128)} %make_tiles.1), calls=%async_computation.1 | async-start | bytes 524288 | tf_op jit(solution)/shard_map/all_to_all | solution.py:288
  25.1 75.4 %all-to-all-start = ((bf16[512,8,128]{2,1,0:T(8,128)(2,1)}), bf16[512,8,128]{2,1,0:T(8,128)(2,1)S(1)}, u32[]{:S(2)}, u32[]{:S(2)}) async-start(bf16[512,8,128]{2,1,0:T(8,128)(2,1)} %bitcast.11), calls=%async_computation | async-start | bytes 2097152 | tf_op jit(solution)/shard_map/all_to_all | solution.py:291

commit v5 on v4

--- a/solution.py
+++ b/solution.py
@@ -175,7 +175,7 @@
     return lax.dot_general(a, b, (((1,), (1,)), ((), ())), preferred_element_type=F32)
 
 
-def prepare_kernel(tile_ref, sel_ref, inv_ref):
+def prepare_kernel(tile_ref, place_ref, sel_ref, inv_ref):
     rows = sel_ref.shape[0]
     tile = tile_ref[...]
     n = tile.shape[1]
@@ -185,7 +185,10 @@
     ids = jnp.where((lane & 7) < 4, ids, -1.0)
     down = lax.broadcasted_iota(jnp.int32, (rows, rows), 0)
     pol = (lane >> 7) & 1
-    spot = ((lane >> 3) & 15) * 32 + (lane & 3) * 8 + ((lane >> 2) & 1) * 2 + (lane >> 8)
+    x = (place_ref[0] - ((lane >> 5) & 3)) & 3
+    y = (place_ref[1] - ((lane >> 3) & 3)) & 3
+    z = (place_ref[2] - (lane & 3)) & 3
+    spot = y * 128 + x * 32 + z * 8 + ((lane >> 2) & 1) * 2 + (lane >> 8)
     move = jnp.where(down == spot[0:1], 1.0, 0.0).astype(BF16)
     moved = jnp.dot(ids.astype(BF16), move, preferred_element_type=F32).astype(jnp.int32)
     source_row = 2 * moved + pol
@@ -202,14 +205,15 @@
     inv_ref[...] = 1.0 / jnp.maximum(nt(left, right), 1.0)
 
 
-def prepare(tile, inputs, interpret=False):
+def prepare(tile, place, inputs, interpret=False):
     return pl.pallas_call(
         prepare_kernel,
         out_shape=(jax.ShapeDtypeStruct((inputs, inputs), BF16), jax.ShapeDtypeStruct((inputs, inputs), F32)),
         interpret=interpret,
         compiler_params=pltpu.CompilerParams(vmem_limit_bytes=24 << 20),
+        in_specs=[pl.BlockSpec(memory_space=pltpu.VMEM), pl.BlockSpec(memory_space=pltpu.SMEM)],
         name="prepare",
-    )(tile)
+    )(tile, place)
 
 
 def correlate_kernel(x_ref, sel_ref, inv_ref, o_ref, s_ref):
@@ -267,29 +271,38 @@
     for q in range(own):
         ids = jnp.where(down == q, row_ref[q], ids)
     block = jnp.concatenate([flag_ref[...], ids.astype(F32)], axis=0)
-    for d in range(o_ref.shape[0]):
-        o_ref[d] = block
-
-
-def make_tiles(flags, station_row, copies, interpret=False):
+    o_ref[...] = block
+
+
+def make_tile(flags, station_row, interpret=False):
     return pl.pallas_call(
         tile_kernel,
-        out_shape=jax.ShapeDtypeStruct((copies, 2 * flags.shape[0], flags.shape[1]), F32),
+        out_shape=jax.ShapeDtypeStruct((2 * flags.shape[0], flags.shape[1]), F32),
         in_specs=[pl.BlockSpec(memory_space=pltpu.VMEM), pl.BlockSpec(memory_space=pltpu.SMEM)],
         interpret=interpret,
-        name="make_tiles",
+        name="make_tile",
     )(flags, station_row)
+
+
+def gather_line(tile, axis):
+    parts = [tile]
+    for shift in range(1, 4):
+        parts.append(lax.ppermute(tile, axis, [(i, (i + shift) % 4) for i in range(4)]))
+    return jnp.concatenate(parts, axis=0)
 
 
 def on_device(voltages, flags, station_row):
     spectra = flags.shape[1]
     z_hi = (2 * lax.axis_index("a") + lax.axis_index("b")).astype(jnp.int32).reshape(1)
-    tile = make_tiles(flags, station_row, 64)
-    tile = lax.all_to_all(tile, ("x", "y", "l"), split_axis=0, concat_axis=0, tiled=True)
     frames = jnp.transpose(voltages[0].reshape(2, -1, 16, 128), (1, 2, 0, 3)).reshape(-1, 128)
+    tile = make_tile(flags, station_row)
     blocks = channelize(frames, flags, z_hi, spectra).reshape(512, 8, spectra)
+    tile, blocks = lax.optimization_barrier((tile, blocks))
     moved = lax.all_to_all(blocks, ("b", "c", "x", "y", "a", "l"), split_axis=0, concat_axis=0, tiled=True)
-    sel, inv = prepare(tile.reshape(512, spectra), 512)
+    for axis in ("l", "x", "y"):
+        tile = gather_line(tile, axis)
+    place = jnp.stack([lax.axis_index(axis) for axis in ("x", "y", "l")]).astype(jnp.int32)
+    sel, inv = prepare(tile, place, 512)
     return correlate(moved.reshape(4096, spectra), sel, inv)
 
 

time: 104 us -> 110 us (1.058)
  the two profiles are of different devices: /device:TPU:1 before, /device:TPU:352 now
where the time goes in v5:
time: 110 us
  starting transfers between devices  53.3 us (48%)
  waiting for transfers between devices  41 us (37%)
  Pallas kernels  15 us (14%)
    ppermute x9, waiting for transfers between devices, gather_line(): lax.ppermute(tile, axis, [(i, (i + shift) % 4) for i in range(4)])  41 us
    ppermute x9, starting transfers between devices, gather_line(): lax.ppermute(tile, axis, [(i, (i + shift) % 4) for i in range(4)])  32.1 us
    all_to_all x1, starting transfers between devices, on_device(): lax.all_to_all(blocks, ('b', 'c', 'x', 'y', 'a', 'l'), split_axis=0, conc...  21.2 us
    pallas_call x1, Pallas kernels, channelize(): pl.pallas_call(channelize_kernel, out_shape=jax.ShapeDtypeStruct((4096, s...  8.47 us
    pallas_call x1, Pallas kernels, correlate(): pl.pallas_call(correlate_kernel, grid=(channels // 2,), in_specs=[pl.Bloc...  3.11 us
  transfers between devices with their start and end apart: 10, of which 5 were waited for; matrix products, arithmetic and copies ran while one was open for 0% of the time, Pallas kernels for 2%

profile of v5, /device:TPU:352, one launch (start us, length us, event | category | flops | bytes accessed | tf_op | source)
XLA Modules:
  0.0 109.6 jit_solution(8623058826531859683)
XLA Ops:
  0.0 1.4 %make_tile.1 = f32[8,128]{1,0:T(8,128)} custom-call(f32[4,128]{1,0:T(4,128)} %w_ref.1, s32[4]{0:T(128)} %row_ref.1), custom_call_target="tpu_custom_call" | custom-call | tf_op jit(solution)/shard_map/make_tile/pallas_call | solution.py:278
  1.4 8.5 %channelize.1 = bf16[4096,128]{1,0:T(8,128)(2,1)} custom-call(bf16[4576,128]{1,0:T(8,128)(2,1)} %bitcast.13, f32[512,128]{1,0:T(8,128)} %constant.30.clone.h_ref, f32[2,16,128]{2,1,0:T(8,128)} %constant.31.clone.tw_ref, bf16[256,256]{1,0:T(8,128)(2,1)} %constant.32.clone.dhi_ref, bf16[256,256]{1,0:T(8,128)(2,1)} %constant.33.clone.dlo_ref, f32[4,128]{1,0:T(4,128)} %w_ref.1, ...), custom_call_target="tpu_custom_call" | custom-call | tf_op jit(solution)/shard_map/channelize/pallas_call | solution.py:157
  9.9 21.2 %all-to-all-start = ((bf16[512,8,128]{2,1,0:T(8,128)(2,1)}), bf16[512,8,128]{2,1,0:T(8,128)(2,1)S(1)}, u32[]{:S(2)}, u32[]{:S(2)}) async-start(bf16[512,8,128]{2,1,0:T(8,128)(2,1)} %bitcast.12), calls=%async_computation | async-start | bytes 2097152 | tf_op jit(solution)/shard_map/all_to_all | solution.py:301
  31.1 3.1 %collective-permute-start.2 = (f32[8,128]{1,0:T(8,128)S(1)}, f32[8,128]{1,0:T(8,128)S(1)}, u32[]{:S(2)}, u32[]{:S(2)}) collective-permute-start(f32[8,128]{1,0:T(8,128)S(1)} %copy-done), channel_id=1, source_target_pairs={{0,96},{32,0},{64,32},{96,64},{1,97},{33,1},{65,33},{97,65},{2,98}... | collective-permute-start | bytes 12296 | tf_op jit(solution)/shard_map/ppermute | solution.py:290
  34.2 3.7 %collective-permute-start.1 = (f32[8,128]{1,0:T(8,128)S(1)}, f32[8,128]{1,0:T(8,128)S(1)}, u32[]{:S(2)}, u32[]{:S(2)}) collective-permute-start(f32[8,128]{1,0:T(8,128)S(1)} %copy-done), channel_id=1, source_target_pairs={{0,64},{32,96},{64,0},{96,32},{1,65},{33,97},{65,1},{97,33},{2,66}... | collective-permute-start | bytes 12296 | tf_op jit(solution)/shard_map/ppermute | solution.py:290
  37.9 3.6 %collective-permute-start = (f32[8,128]{1,0:T(8,128)S(1)}, f32[8,128]{1,0:T(8,128)S(1)}, u32[]{:S(2)}, u32[]{:S(2)}) collective-permute-start(f32[8,128]{1,0:T(8,128)S(1)} %copy-done), channel_id=1, source_target_pairs={{0,32},{32,64},{64,96},{96,0},{1,33},{33,65},{65,97},{97,1},{2,34}... | collective-permute-start | bytes 12296 | tf_op jit(solution)/shard_map/ppermute | solution.py:290
  41.6 31.3 %collective-permute-done = f32[8,128]{1,0:T(8,128)S(1)} collective-permute-done((f32[8,128]{1,0:T(8,128)S(1)}, f32[8,128]{1,0:T(8,128)S(1)}, u32[]{:S(2)}, u32[]{:S(2)}) %collective-permute-start) | collective-permute-done | bytes 4128 | tf_op jit(solution)/shard_map/ppermute | solution.py:290
  72.9 2.0 %collective-permute-done.1 = f32[8,128]{1,0:T(8,128)S(1)} collective-permute-done((f32[8,128]{1,0:T(8,128)S(1)}, f32[8,128]{1,0:T(8,128)S(1)}, u32[]{:S(2)}, u32[]{:S(2)}) %collective-permute-start.1) | collective-permute-done | bytes 4128 | tf_op jit(solution)/shard_map/ppermute | solution.py:290
  74.9 0.5 collective-permute-done.2
  75.4 3.4 %collective-permute-start.3 = (f32[32,128]{1,0:T(8,128)S(1)}, f32[32,128]{1,0:T(8,128)S(1)}, u32[]{:S(2)}, u32[]{:S(2)}) collective-permute-start(f32[32,128]{1,0:T(8,128)S(1)} %get-tuple-element.21), channel_id=1, source_target_pairs={{0,128},{128,256},{256,384},{384,0},{1,129},{129,257},{257,385},{3... | collective-permute-start | bytes 49160 | tf_op jit(solution)/shard_map/ppermute | solution.py:290
  78.9 3.6 %collective-permute-start.5 = (f32[32,128]{1,0:T(8,128)S(1)}, f32[32,128]{1,0:T(8,128)S(1)}, u32[]{:S(2)}, u32[]{:S(2)}) collective-permute-start(f32[32,128]{1,0:T(8,128)S(1)} %get-tuple-element.21), channel_id=1, source_target_pairs={{0,384},{128,0},{256,128},{384,256},{1,385},{129,1},{257,129},{385... | collective-permute-start | bytes 49160 | tf_op jit(solution)/shard_map/ppermute | solution.py:290
  82.5 3.7 %collective-permute-start.4 = (f32[32,128]{1,0:T(8,128)S(1)}, f32[32,128]{1,0:T(8,128)S(1)}, u32[]{:S(2)}, u32[]{:S(2)}) collective-permute-start(f32[32,128]{1,0:T(8,128)S(1)} %get-tuple-element.21), channel_id=1, source_target_pairs={{0,256},{128,384},{256,0},{384,128},{1,257},{129,385},{257,1},{385... | collective-permute-start | bytes 49160 | tf_op jit(solution)/shard_map/ppermute | solution.py:290
  86.2 0.0 collective-permute-done.3
  86.2 3.4 %collective-permute-done.4 = f32[32,128]{1,0:T(8,128)S(1)} collective-permute-done((f32[32,128]{1,0:T(8,128)S(1)}, f32[32,128]{1,0:T(8,128)S(1)}, u32[]{:S(2)}, u32[]{:S(2)}) %collective-permute-start.4) | collective-permute-done | bytes 16416 | tf_op jit(solution)/shard_map/ppermute | solution.py:290
  89.6 0.0 collective-permute-done.5
  89.6 3.4 %collective-permute-start.6 = (f32[128,128]{1,0:T(8,128)S(1)}, f32[128,128]{1,0:T(8,128)S(1)}, u32[]{:S(2)}, u32[]{:S(2)}) collective-permute-start(f32[128,128]{1,0:T(8,128)S(1)} %get-tuple-element.13), channel_id=1, source_target_pairs={{0,8},{8,16},{16,24},{24,0},{1,9},{9,17},{17,25},{25,1},{2,10},{10... | collective-permute-start | bytes 196616 | tf_op jit(solution)/shard_map/ppermute | solution.py:290
  93.1 0.1 pad_add_fusion.place_ref
  93.2 3.6 %collective-permute-start.8 = (f32[128,128]{1,0:T(8,128)S(1)}, f32[128,128]{1,0:T(8,128)S(1)}, u32[]{:S(2)}, u32[]{:S(2)}) collective-permute-start(f32[128,128]{1,0:T(8,128)S(1)} %get-tuple-element.13), channel_id=1, source_target_pairs={{0,24},{8,0},{16,8},{24,16},{1,25},{9,1},{17,9},{25,17},{2,26},{10... | collective-permute-start | bytes 196616 | tf_op jit(solution)/shard_map/ppermute | solution.py:290
  96.8 3.8 %collective-permute-start.7 = (f32[128,128]{1,0:T(8,128)S(1)}, f32[128,128]{1,0:T(8,128)S(1)}, u32[]{:S(2)}, u32[]{:S(2)}) collective-permute-start(f32[128,128]{1,0:T(8,128)S(1)} %get-tuple-element.13), channel_id=1, source_target_pairs={{0,16},{8,24},{16,0},{24,8},{1,17},{9,25},{17,1},{25,9},{2,18},{10... | collective-permute-start | bytes 196616 | tf_op jit(solution)/shard_map/ppermute | solution.py:290
  100.7 3.8 %collective-permute-done.7 = f32[128,128]{1,0:T(8,128)S(1)} collective-permute-done((f32[128,128]{1,0:T(8,128)S(1)}, f32[128,128]{1,0:T(8,128)S(1)}, u32[]{:S(2)}, u32[]{:S(2)}) %collective-permute-start.7) | collective-permute-done | bytes 65568 | tf_op jit(solution)/shard_map/ppermute | solution.py:290
  104.4 0.0 collective-permute-done.8
  104.5 2.0 %prepare.1 = (bf16[512,512]{1,0:T(8,128)(2,1)S(1)}, f32[512,512]{1,0:T(8,128)S(1)}) custom-call(f32[512,128]{1,0:T(8,128)S(1)} %constant_dynamic-update-slice_fusion.11.tile_ref, s32[3]{0:T(128)S(1)} %pad_add_fusion.place_ref), custom_call_target="tpu_custom_call" | custom-call | tf_op jit(solution)/shard_map/prepare/pallas_call | solution.py:209
  106.4 0.0 all-to-all-done
  106.5 3.1 %correlate.1 = bf16[4,512,512]{2,1,0:T(8,128)(2,1)} custom-call(bf16[4096,128]{1,0:T(8,128)(2,1)S(1)} %bitcast.11, bf16[512,512]{1,0:T(8,128)(2,1)S(1)} %get-tuple-element.11.sel_ref, f32[512,512]{1,0:T(8,128)S(1)} %get-tuple-element.12.inv_ref), custom_call_target="tpu_custom_call" | custom-call | tf_op jit(solution)/shard_map/correlate/pallas_call | solution.py:254
  (13 shorter events, 0.0 us)
Async XLA Ops:
  1.4 29.7 %copy-start = (f32[8,128]{1,0:T(8,128)S(1)}, f32[8,128]{1,0:T(8,128)}, u32[]{:S(2)}) copy-start(f32[8,128]{1,0:T(8,128)} %make_tile.1) | copy-start | bytes 12292
  9.9 96.6 %all-to-all-start = ((bf16[512,8,128]{2,1,0:T(8,128)(2,1)}), bf16[512,8,128]{2,1,0:T(8,128)(2,1)S(1)}, u32[]{:S(2)}, u32[]{:S(2)}) async-start(bf16[512,8,128]{2,1,0:T(8,128)(2,1)} %bitcast.12), calls=%async_computation | async-start | bytes 2097152 | tf_op jit(solution)/shard_map/all_to_all | solution.py:301
  31.1 44.3 %collective-permute-start.2 = (f32[8,128]{1,0:T(8,128)S(1)}, f32[8,128]{1,0:T(8,128)S(1)}, u32[]{:S(2)}, u32[]{:S(2)}) collective-permute-start(f32[8,128]{1,0:T(8,128)S(1)} %copy-done), channel_id=1, source_target_pairs={{0,96},{32,0},{64,32},{96,64},{1,97},{33,1},{65,33},{97,65},{2,98}... | collective-permute-start | bytes 12296 | tf_op jit(solution)/shard_map/ppermute | solution.py:290
  34.2 40.7 %collective-permute-start.1 = (f32[8,128]{1,0:T(8,128)S(1)}, f32[8,128]{1,0:T(8,128)S(1)}, u32[]{:S(2)}, u32[]{:S(2)}) collective-permute-start(f32[8,128]{1,0:T(8,128)S(1)} %copy-done), channel_id=1, source_target_pairs={{0,64},{32,96},{64,0},{96,32},{1,65},{33,97},{65,1},{97,33},{2,66}... | collective-permute-start | bytes 12296 | tf_op jit(solution)/shard_map/ppermute | solution.py:290
  37.9 35.0 %collective-permute-start = (f32[8,128]{1,0:T(8,128)S(1)}, f32[8,128]{1,0:T(8,128)S(1)}, u32[]{:S(2)}, u32[]{:S(2)}) collective-permute-start(f32[8,128]{1,0:T(8,128)S(1)} %copy-done), channel_id=1, source_target_pairs={{0,32},{32,64},{64,96},{96,0},{1,33},{33,65},{65,97},{97,1},{2,34}... | collective-permute-start | bytes 12296 | tf_op jit(solution)/shard_map/ppermute | solution.py:290
  75.4 10.8 %collective-permute-start.3 = (f32[32,128]{1,0:T(8,128)S(1)}, f32[32,128]{1,0:T(8,128)S(1)}, u32[]{:S(2)}, u32[]{:S(2)}) collective-permute-start(f32[32,128]{1,0:T(8,128)S(1)} %get-tuple-element.21), channel_id=1, source_target_pairs={{0,128},{128,256},{256,384},{384,0},{1,129},{129,257},{257,385},{3... | collective-permute-start | bytes 49160 | tf_op jit(solution)/shard_map/ppermute | solution.py:290
  78.9 10.8 %collective-permute-start.5 = (f32[32,128]{1,0:T(8,128)S(1)}, f32[32,128]{1,0:T(8,128)S(1)}, u32[]{:S(2)}, u32[]{:S(2)}) collective-permute-start(f32[32,128]{1,0:T(8,128)S(1)} %get-tuple-element.21), channel_id=1, source_target_pairs={{0,384},{128,0},{256,128},{384,256},{1,385},{129,1},{257,129},{385... | collective-permute-start | bytes 49160 | tf_op jit(solution)/shard_map/ppermute | solution.py:290
  82.5 7.1 %collective-permute-start.4 = (f32[32,128]{1,0:T(8,128)S(1)}, f32[32,128]{1,0:T(8,128)S(1)}, u32[]{:S(2)}, u32[]{:S(2)}) collective-permute-start(f32[32,128]{1,0:T(8,128)S(1)} %get-tuple-element.21), channel_id=1, source_target_pairs={{0,256},{128,384},{256,0},{384,128},{1,257},{129,385},{257,1},{385... | collective-permute-start | bytes 49160 | tf_op jit(solution)/shard_map/ppermute | solution.py:290
  89.6 11.0 %collective-permute-start.6 = (f32[128,128]{1,0:T(8,128)S(1)}, f32[128,128]{1,0:T(8,128)S(1)}, u32[]{:S(2)}, u32[]{:S(2)}) collective-permute-start(f32[128,128]{1,0:T(8,128)S(1)} %get-tuple-element.13), channel_id=1, source_target_pairs={{0,8},{8,16},{16,24},{24,0},{1,9},{9,17},{17,25},{25,1},{2,10},{10... | collective-permute-start | bytes 196616 | tf_op jit(solution)/shard_map/ppermute | solution.py:290
  93.2 11.3 %collective-permute-start.8 = (f32[128,128]{1,0:T(8,128)S(1)}, f32[128,128]{1,0:T(8,128)S(1)}, u32[]{:S(2)}, u32[]{:S(2)}) collective-permute-start(f32[128,128]{1,0:T(8,128)S(1)} %get-tuple-element.13), channel_id=1, source_target_pairs={{0,24},{8,0},{16,8},{24,16},{1,25},{9,1},{17,9},{25,17},{2,26},{10... | collective-permute-start | bytes 196616 | tf_op jit(solution)/shard_map/ppermute | solution.py:290
  96.8 7.7 %collective-permute-start.7 = (f32[128,128]{1,0:T(8,128)S(1)}, f32[128,128]{1,0:T(8,128)S(1)}, u32[]{:S(2)}, u32[]{:S(2)}) collective-permute-start(f32[128,128]{1,0:T(8,128)S(1)} %get-tuple-element.13), channel_id=1, source_target_pairs={{0,16},{8,24},{16,0},{24,8},{1,17},{9,25},{17,1},{25,9},{2,18},{10... | collective-permute-start | bytes 196616 | tf_op jit(solution)/shard_map/ppermute | solution.py:290

commit v6 on v5

--- a/solution.py
+++ b/solution.py
@@ -187,7 +187,7 @@
     pol = (lane >> 7) & 1
     x = (place_ref[0] - ((lane >> 5) & 3)) & 3
     y = (place_ref[1] - ((lane >> 3) & 3)) & 3
-    z = (place_ref[2] - (lane & 3)) & 3
+    z = lane & 3
     spot = y * 128 + x * 32 + z * 8 + ((lane >> 2) & 1) * 2 + (lane >> 8)
     move = jnp.where(down == spot[0:1], 1.0, 0.0).astype(BF16)
     moved = jnp.dot(ids.astype(BF16), move, preferred_element_type=F32).astype(jnp.int32)
@@ -271,16 +271,17 @@
     for q in range(own):
         ids = jnp.where(down == q, row_ref[q], ids)
     block = jnp.concatenate([flag_ref[...], ids.astype(F32)], axis=0)
-    o_ref[...] = block
-
-
-def make_tile(flags, station_row, interpret=False):
+    for d in range(o_ref.shape[0]):
+        o_ref[d] = block
+
+
+def make_tiles(flags, station_row, copies, interpret=False):
     return pl.pallas_call(
         tile_kernel,
-        out_shape=jax.ShapeDtypeStruct((2 * flags.shape[0], flags.shape[1]), F32),
+        out_shape=jax.ShapeDtypeStruct((copies, 2 * flags.shape[0], flags.shape[1]), F32),
         in_specs=[pl.BlockSpec(memory_space=pltpu.VMEM), pl.BlockSpec(memory_space=pltpu.SMEM)],
         interpret=interpret,
-        name="make_tile",
+        name="make_tiles",
     )(flags, station_row)
 
 
@@ -295,13 +296,14 @@
     spectra = flags.shape[1]
     z_hi = (2 * lax.axis_index("a") + lax.axis_index("b")).astype(jnp.int32).reshape(1)
     frames = jnp.transpose(voltages[0].reshape(2, -1, 16, 128), (1, 2, 0, 3)).reshape(-1, 128)
-    tile = make_tile(flags, station_row)
+    tile = make_tiles(flags, station_row, 4)
+    tile = lax.all_to_all(tile, "l", split_axis=0, concat_axis=0, tiled=True).reshape(32, spectra)
     blocks = channelize(frames, flags, z_hi, spectra).reshape(512, 8, spectra)
     tile, blocks = lax.optimization_barrier((tile, blocks))
     moved = lax.all_to_all(blocks, ("b", "c", "x", "y", "a", "l"), split_axis=0, concat_axis=0, tiled=True)
-    for axis in ("l", "x", "y"):
+    for axis in ("x", "y"):
         tile = gather_line(tile, axis)
-    place = jnp.stack([lax.axis_index(axis) for axis in ("x", "y", "l")]).astype(jnp.int32)
+    place = jnp.stack([lax.axis_index(axis) for axis in ("x", "y")]).astype(jnp.int32)
     sel, inv = prepare(tile, place, 512)
     return correlate(moved.reshape(4096, spectra), sel, inv)
 

time: 110 us -> 97.9 us (0.89)
  the two profiles are of different devices: /device:TPU:352 before, /device:TPU:1 now
where the time goes in v6:
time: 97.9 us; the launch traced here: 97.5 us
  starting transfers between devices  47.2 us (48%)
  waiting for transfers between devices  35.2 us (36%)
  Pallas kernels  14.9 us (15%)
    all_to_all x1, waiting for transfers between devices, on_device(): lax.all_to_all(blocks, ('b', 'c', 'x', 'y', 'a', 'l'), split_axis=0, conc...  27.4 us
    all_to_all x1, starting transfers between devices, on_device(): lax.all_to_all(blocks, ('b', 'c', 'x', 'y', 'a', 'l'), split_axis=0, conc...  21.6 us
    ppermute x6, starting transfers between devices, gather_line(): lax.ppermute(tile, axis, [(i, (i + shift) % 4) for i in range(4)])  19.1 us
    pallas_call x1, Pallas kernels, channelize(): pl.pallas_call(channelize_kernel, out_shape=jax.ShapeDtypeStruct((4096, s...  8.47 us
    ppermute x6, waiting for transfers between devices, gather_line(): lax.ppermute(tile, axis, [(i, (i + shift) % 4) for i in range(4)])  7.71 us
    all_to_all x1, starting transfers between devices, on_device(): lax.all_to_all(tile, 'l', split_axis=0, concat_axis=0, tiled=True)  6.43 us
    pallas_call x1, Pallas kernels, correlate(): pl.pallas_call(correlate_kernel, grid=(channels // 2,), in_specs=[pl.Bloc...  3.07 us
    pallas_call x1, Pallas kernels, prepare(): pl.pallas_call(prepare_kernel, out_shape=(jax.ShapeDtypeStruct((inputs, i...  1.97 us
  transfers between devices with their start and end apart: 8, of which 3 were waited for; matrix products, arithmetic and copies ran while one was open for 0% of the time, Pallas kernels for 11%

profile of v6, /device:TPU:1, one launch (start us, length us, event | category | flops | bytes accessed | tf_op | source)
XLA Modules:
  0.0 97.5 jit_solution(1766404841302177995)
XLA Ops:
  0.0 1.4 %make_tiles.1 = f32[4,8,128]{2,1,0:T(8,128)} custom-call(f32[4,128]{1,0:T(4,128)} %w_ref.1, s32[4]{0:T(128)} %row_ref.1), custom_call_target="tpu_custom_call" | custom-call | tf_op jit(solution)/shard_map/make_tiles/pallas_call | solution.py:279
  1.4 6.4 %all-to-all-start = ((f32[4,8,128]{2,1,0:T(8,128)}), f32[4,8,128]{2,1,0:T(8,128)S(1)}, u32[]{:S(2)}, u32[]{:S(2)}) async-start(f32[4,8,128]{2,1,0:T(8,128)} %make_tiles.1), calls=%async_computation | async-start | bytes 32768 | tf_op jit(solution)/shard_map/all_to_all | solution.py:300
  7.8 8.5 %channelize.1 = bf16[4096,128]{1,0:T(8,128)(2,1)} custom-call(bf16[4576,128]{1,0:T(8,128)(2,1)} %bitcast.13, f32[512,128]{1,0:T(8,128)} %constant.26.clone.h_ref, f32[2,16,128]{2,1,0:T(8,128)} %constant.27.clone.tw_ref, bf16[256,256]{1,0:T(8,128)(2,1)} %constant.28.clone.dhi_ref, bf16[256,256]{1,0:T(8,128)(2,1)} %constant.29.clone.dlo_ref, f32[4,128]{1,0:T(4,128)} %w_ref.1, ...), custom_call_target="tpu_custom_call" | custom-call | tf_op jit(solution)/shard_map/channelize/pallas_call | solution.py:157
  16.3 0.0 all-to-all-done
  16.3 21.6 %all-to-all-start.1 = ((bf16[512,8,128]{2,1,0:T(8,128)(2,1)}), bf16[512,8,128]{2,1,0:T(8,128)(2,1)S(1)}, u32[]{:S(2)}, u32[]{:S(2)}) async-start(bf16[512,8,128]{2,1,0:T(8,128)(2,1)} %bitcast.12), calls=%async_computation.1 | async-start | bytes 2097152 | tf_op jit(solution)/shard_map/all_to_all | solution.py:303
  38.0 4.5 %collective-permute-start.2 = (f32[32,128]{1,0:T(8,128)S(1)}, f32[32,128]{1,0:T(8,128)S(1)}, u32[]{:S(2)}, u32[]{:S(2)}) collective-permute-start(f32[32,128]{1,0:T(8,128)S(1)} %bitcast.14), channel_id=1, source_target_pairs={{0,384},{128,0},{256,128},{384,256},{1,385},{129,1},{257,129},{385... | collective-permute-start | bytes 49160 | tf_op jit(solution)/shard_map/ppermute | solution.py:291
  42.4 2.5 %collective-permute-start.1 = (f32[32,128]{1,0:T(8,128)S(1)}, f32[32,128]{1,0:T(8,128)S(1)}, u32[]{:S(2)}, u32[]{:S(2)}) collective-permute-start(f32[32,128]{1,0:T(8,128)S(1)} %bitcast.15), channel_id=1, source_target_pairs={{0,256},{128,384},{256,0},{384,128},{1,257},{129,385},{257,1},{385... | collective-permute-start | bytes 49160 | tf_op jit(solution)/shard_map/ppermute | solution.py:291
  44.9 2.5 %collective-permute-start = (f32[32,128]{1,0:T(8,128)S(1)}, f32[32,128]{1,0:T(8,128)S(1)}, u32[]{:S(2)}, u32[]{:S(2)}) collective-permute-start(f32[32,128]{1,0:T(8,128)S(1)} %bitcast.16), channel_id=1, source_target_pairs={{0,128},{128,256},{256,384},{384,0},{1,129},{129,257},{257,385},{3... | collective-permute-start | bytes 49160 | tf_op jit(solution)/shard_map/ppermute | solution.py:291
  47.4 3.7 %collective-permute-done = f32[32,128]{1,0:T(8,128)S(1)} collective-permute-done((f32[32,128]{1,0:T(8,128)S(1)}, f32[32,128]{1,0:T(8,128)S(1)}, u32[]{:S(2)}, u32[]{:S(2)}) %collective-permute-start) | collective-permute-done | bytes 16416 | tf_op jit(solution)/shard_map/ppermute | solution.py:291
  51.2 0.0 collective-permute-done.1
  51.2 0.0 collective-permute-done.2
  51.2 2.8 %collective-permute-start.3 = (f32[128,128]{1,0:T(8,128)S(1)}, f32[128,128]{1,0:T(8,128)S(1)}, u32[]{:S(2)}, u32[]{:S(2)}) collective-permute-start(f32[128,128]{1,0:T(8,128)S(1)} %get-tuple-element.13), channel_id=1, source_target_pairs={{0,8},{8,16},{16,24},{24,0},{1,9},{9,17},{17,25},{25,1},{2,10},{10... | collective-permute-start | bytes 196616 | tf_op jit(solution)/shard_map/ppermute | solution.py:291
  54.1 0.1 pad_add_fusion.place_ref
  54.1 3.6 %collective-permute-start.5 = (f32[128,128]{1,0:T(8,128)S(1)}, f32[128,128]{1,0:T(8,128)S(1)}, u32[]{:S(2)}, u32[]{:S(2)}) collective-permute-start(f32[128,128]{1,0:T(8,128)S(1)} %get-tuple-element.13), channel_id=1, source_target_pairs={{0,24},{8,0},{16,8},{24,16},{1,25},{9,1},{17,9},{25,17},{2,26},{10... | collective-permute-start | bytes 196616 | tf_op jit(solution)/shard_map/ppermute | solution.py:291
  57.8 3.2 %collective-permute-start.4 = (f32[128,128]{1,0:T(8,128)S(1)}, f32[128,128]{1,0:T(8,128)S(1)}, u32[]{:S(2)}, u32[]{:S(2)}) collective-permute-start(f32[128,128]{1,0:T(8,128)S(1)} %get-tuple-element.13), channel_id=1, source_target_pairs={{0,16},{8,24},{16,0},{24,8},{1,17},{9,25},{17,1},{25,9},{2,18},{10... | collective-permute-start | bytes 196616 | tf_op jit(solution)/shard_map/ppermute | solution.py:291
  61.0 0.0 collective-permute-done.3
  61.0 4.0 %collective-permute-done.4 = f32[128,128]{1,0:T(8,128)S(1)} collective-permute-done((f32[128,128]{1,0:T(8,128)S(1)}, f32[128,128]{1,0:T(8,128)S(1)}, u32[]{:S(2)}, u32[]{:S(2)}) %collective-permute-start.4) | collective-permute-done | bytes 65568 | tf_op jit(solution)/shard_map/ppermute | solution.py:291
  65.0 0.0 collective-permute-done.5
  65.0 2.0 %prepare.1 = (bf16[512,512]{1,0:T(8,128)(2,1)S(1)}, f32[512,512]{1,0:T(8,128)S(1)}) custom-call(f32[512,128]{1,0:T(8,128)S(1)} %constant_dynamic-update-slice_fusion.4.tile_ref, s32[2]{0:T(128)S(1)} %pad_add_fusion.place_ref), custom_call_target="tpu_custom_call" | custom-call | tf_op jit(solution)/shard_map/prepare/pallas_call | solution.py:209
  67.0 27.4 %all-to-all-done.1 = bf16[512,8,128]{2,1,0:T(8,128)(2,1)S(1)} async-done(((bf16[512,8,128]{2,1,0:T(8,128)(2,1)}), bf16[512,8,128]{2,1,0:T(8,128)(2,1)S(1)}, u32[]{:S(2)}, u32[]{:S(2)}) %all-to-all-start.1) | async-done | bytes 1048608 | tf_op jit(solution)/shard_map/all_to_all | solution.py:303
  94.4 3.1 %correlate.1 = bf16[4,512,512]{2,1,0:T(8,128)(2,1)} custom-call(bf16[4096,128]{1,0:T(8,128)(2,1)S(1)} %bitcast.11, bf16[512,512]{1,0:T(8,128)(2,1)S(1)} %get-tuple-element.11.sel_ref, f32[512,512]{1,0:T(8,128)S(1)} %get-tuple-element.12.inv_ref), custom_call_target="tpu_custom_call" | custom-call | tf_op jit(solution)/shard_map/correlate/pallas_call | solution.py:254
  (7 shorter events, 0.0 us)
Async XLA Ops:
  1.4 14.9 %all-to-all-start = ((f32[4,8,128]{2,1,0:T(8,128)}), f32[4,8,128]{2,1,0:T(8,128)S(1)}, u32[]{:S(2)}, u32[]{:S(2)}) async-start(f32[4,8,128]{2,1,0:T(8,128)} %make_tiles.1), calls=%async_computation | async-start | bytes 32768 | tf_op jit(solution)/shard_map/all_to_all | solution.py:300
  16.3 78.1 %all-to-all-start.1 = ((bf16[512,8,128]{2,1,0:T(8,128)(2,1)}), bf16[512,8,128]{2,1,0:T(8,128)(2,1)S(1)}, u32[]{:S(2)}, u32[]{:S(2)}) async-start(bf16[512,8,128]{2,1,0:T(8,128)(2,1)} %bitcast.12), calls=%async_computation.1 | async-start | bytes 2097152 | tf_op jit(solution)/shard_map/all_to_all | solution.py:303
  38.0 13.2 %collective-permute-start.2 = (f32[32,128]{1,0:T(8,128)S(1)}, f32[32,128]{1,0:T(8,128)S(1)}, u32[]{:S(2)}, u32[]{:S(2)}) collective-permute-start(f32[32,128]{1,0:T(8,128)S(1)} %bitcast.14), channel_id=1, source_target_pairs={{0,384},{128,0},{256,128},{384,256},{1,385},{129,1},{257,129},{385... | collective-permute-start | bytes 49160 | tf_op jit(solution)/shard_map/ppermute | solution.py:291
  42.4 8.7 %collective-permute-start.1 = (f32[32,128]{1,0:T(8,128)S(1)}, f32[32,128]{1,0:T(8,128)S(1)}, u32[]{:S(2)}, u32[]{:S(2)}) collective-permute-start(f32[32,128]{1,0:T(8,128)S(1)} %bitcast.15), channel_id=1, source_target_pairs={{0,256},{128,384},{256,0},{384,128},{1,257},{129,385},{257,1},{385... | collective-permute-start | bytes 49160 | tf_op jit(solution)/shard_map/ppermute | solution.py:291
  44.9 6.2 %collective-permute-start = (f32[32,128]{1,0:T(8,128)S(1)}, f32[32,128]{1,0:T(8,128)S(1)}, u32[]{:S(2)}, u32[]{:S(2)}) collective-permute-start(f32[32,128]{1,0:T(8,128)S(1)} %bitcast.16), channel_id=1, source_target_pairs={{0,128},{128,256},{256,384},{384,0},{1,129},{129,257},{257,385},{3... | collective-permute-start | bytes 49160 | tf_op jit(solution)/shard_map/ppermute | solution.py:291
  51.2 9.8 %collective-permute-start.3 = (f32[128,128]{1,0:T(8,128)S(1)}, f32[128,128]{1,0:T(8,128)S(1)}, u32[]{:S(2)}, u32[]{:S(2)}) collective-permute-start(f32[128,128]{1,0:T(8,128)S(1)} %get-tuple-element.13), channel_id=1, source_target_pairs={{0,8},{8,16},{16,24},{24,0},{1,9},{9,17},{17,25},{25,1},{2,10},{10... | collective-permute-start | bytes 196616 | tf_op jit(solution)/shard_map/ppermute | solution.py:291
  54.1 10.8 %collective-permute-start.5 = (f32[128,128]{1,0:T(8,128)S(1)}, f32[128,128]{1,0:T(8,128)S(1)}, u32[]{:S(2)}, u32[]{:S(2)}) collective-permute-start(f32[128,128]{1,0:T(8,128)S(1)} %get-tuple-element.13), channel_id=1, source_target_pairs={{0,24},{8,0},{16,8},{24,16},{1,25},{9,1},{17,9},{25,17},{2,26},{10... | collective-permute-start | bytes 196616 | tf_op jit(solution)/shard_map/ppermute | solution.py:291
  57.8 7.2 %collective-permute-start.4 = (f32[128,128]{1,0:T(8,128)S(1)}, f32[128,128]{1,0:T(8,128)S(1)}, u32[]{:S(2)}, u32[]{:S(2)}) collective-permute-start(f32[128,128]{1,0:T(8,128)S(1)} %get-tuple-element.13), channel_id=1, source_target_pairs={{0,16},{8,24},{16,0},{24,8},{1,17},{9,25},{17,1},{25,9},{2,18},{10... | collective-permute-start | bytes 196616 | tf_op jit(solution)/shard_map/ppermute | solution.py:291

commit v7 on v6

--- a/solution.py
+++ b/solution.py
@@ -125,22 +125,19 @@
 
     lax.fori_loop(0, spectra // 16, mix, 0)
 
-    def turn(q, _):
-        def dot(a, b):
-            return lax.dot_general(a, b, (((1,), (1,)), ((), ())), preferred_element_type=F32)
-
-        weight = w_ref[pl.ds(z_ref[0], 1), :]
-        dhi, dlo = dhi_ref[...], dlo_ref[...]
+    def dot(a, b):
+        return lax.dot_general(a, b, (((1,), (1,)), ((), ())), preferred_element_type=F32)
+
+    weight = w_ref[pl.ds(z_ref[0], 1), :]
+    dhi, dlo = dhi_ref[...], dlo_ref[...]
+    for q in range(4):
         for i in range(4):
-            hi, lo = ahi_ref[4 * q + i], alo_ref[4 * q + i]
-            out = dot(dhi, hi) + (dot(dhi, lo) + dot(dlo, hi))
+            hi = ahi_ref[4 * q + i]
+            out = dot(dhi, hi) + (dot(dhi, alo_ref[4 * q + i]) + dot(dlo, hi))
             out = out.astype(BF16).astype(F32) * weight
             for c in range(2):
-                m_ref[pl.ds(2 * i + c, 128, stride=8), :] = out[128 * c : 128 * (c + 1)]
-        o_ref[pl.ds(pl.multiple_of(q * 1024, 1024), 1024), :] = m_ref[...].astype(BF16)
-        return 0
-
-    lax.fori_loop(0, 4, turn, 0)
+                m_ref[pl.ds(1024 * q + 2 * i + c, 128, stride=8), :] = out[128 * c : 128 * (c + 1)]
+        o_ref[1024 * q : 1024 * (q + 1), :] = m_ref[1024 * q : 1024 * (q + 1), :].astype(BF16)
 
 
 def channelize(voltages, flags, station, spectra, interpret=False):
@@ -163,7 +160,7 @@
             pltpu.VMEM((2, 16, spectra, 128), F32),
             pltpu.VMEM((16, spectra, 256), BF16),
             pltpu.VMEM((16, spectra, 256), BF16),
-            pltpu.VMEM((1024, spectra), F32),
+            pltpu.VMEM((4096, spectra), F32),
         ],
         in_specs=[pl.BlockSpec(memory_space=pltpu.VMEM)] * 6 + [pl.BlockSpec(memory_space=pltpu.SMEM)],
         interpret=interpret,

time: 97.9 us -> 97.4 us (level)
  transfers between devices with their start and end apart: 8 -> 8, of which waited for: 3 -> 3; matrix products, arithmetic and copies ran while one was open for 0% -> 0% of each run, Pallas kernels for 11% -> 10%
where the time goes in v7:
time: 97.4 us; the launch traced here: 97 us
  starting transfers between devices  47.2 us (48%)
  waiting for transfers between devices  35.1 us (36%)
  Pallas kernels  14.4 us (15%)
    all_to_all x1, waiting for transfers between devices, on_device(): lax.all_to_all(blocks, ('b', 'c', 'x', 'y', 'a', 'l'), split_axis=0, conc...  27.4 us
    all_to_all x1, starting transfers between devices, on_device(): lax.all_to_all(blocks, ('b', 'c', 'x', 'y', 'a', 'l'), split_axis=0, conc...  21.6 us
    ppermute x6, starting transfers between devices, gather_line(): lax.ppermute(tile, axis, [(i, (i + shift) % 4) for i in range(4)])  19.1 us
    pallas_call x1, Pallas kernels, channelize(): pl.pallas_call(channelize_kernel, out_shape=jax.ShapeDtypeStruct((4096, s...  7.95 us
    ppermute x6, waiting for transfers between devices, gather_line(): lax.ppermute(tile, axis, [(i, (i + shift) % 4) for i in range(4)])  7.71 us
    all_to_all x1, starting transfers between devices, on_device(): lax.all_to_all(tile, 'l', split_axis=0, concat_axis=0, tiled=True)  6.43 us
    pallas_call x1, Pallas kernels, correlate(): pl.pallas_call(correlate_kernel, grid=(channels // 2,), in_specs=[pl.Bloc...  3.08 us
    pallas_call x1, Pallas kernels, prepare(): pl.pallas_call(prepare_kernel, out_shape=(jax.ShapeDtypeStruct((inputs, i...  1.97 us
  transfers between devices with their start and end apart: 8, of which 3 were waited for; matrix products, arithmetic and copies ran while one was open for 0% of the time, Pallas kernels for 10%

profile of v7, /device:TPU:1, one launch (start us, length us, event | category | flops | bytes accessed | tf_op | source)
XLA Modules:
  0.0 97.0 jit_solution(465583004509284689)
XLA Ops:
  0.0 1.4 %make_tiles.1 = f32[4,8,128]{2,1,0:T(8,128)} custom-call(f32[4,128]{1,0:T(4,128)} %w_ref.1, s32[4]{0:T(128)} %row_ref.1), custom_call_target="tpu_custom_call" | custom-call | tf_op jit(solution)/shard_map/make_tiles/pallas_call | solution.py:276
  1.4 6.4 %all-to-all-start = ((f32[4,8,128]{2,1,0:T(8,128)}), f32[4,8,128]{2,1,0:T(8,128)S(1)}, u32[]{:S(2)}, u32[]{:S(2)}) async-start(f32[4,8,128]{2,1,0:T(8,128)} %make_tiles.1), calls=%async_computation | async-start | bytes 32768 | tf_op jit(solution)/shard_map/all_to_all | solution.py:297
  7.8 7.9 %channelize.1 = bf16[4096,128]{1,0:T(8,128)(2,1)} custom-call(bf16[4576,128]{1,0:T(8,128)(2,1)} %bitcast.13, f32[512,128]{1,0:T(8,128)} %constant.26.clone.h_ref, f32[2,16,128]{2,1,0:T(8,128)} %constant.27.clone.tw_ref, bf16[256,256]{1,0:T(8,128)(2,1)} %constant.28.clone.dhi_ref, bf16[256,256]{1,0:T(8,128)(2,1)} %constant.29.clone.dlo_ref, f32[4,128]{1,0:T(4,128)} %w_ref.1, ...), custom_call_target="tpu_custom_call" | custom-call | tf_op jit(solution)/shard_map/channelize/pallas_call | solution.py:154
  15.8 0.0 all-to-all-done
  15.8 21.6 %all-to-all-start.1 = ((bf16[512,8,128]{2,1,0:T(8,128)(2,1)}), bf16[512,8,128]{2,1,0:T(8,128)(2,1)S(1)}, u32[]{:S(2)}, u32[]{:S(2)}) async-start(bf16[512,8,128]{2,1,0:T(8,128)(2,1)} %bitcast.12), calls=%async_computation.1 | async-start | bytes 2097152 | tf_op jit(solution)/shard_map/all_to_all | solution.py:300
  37.4 4.5 %collective-permute-start.2 = (f32[32,128]{1,0:T(8,128)S(1)}, f32[32,128]{1,0:T(8,128)S(1)}, u32[]{:S(2)}, u32[]{:S(2)}) collective-permute-start(f32[32,128]{1,0:T(8,128)S(1)} %bitcast.14), channel_id=1, source_target_pairs={{0,384},{128,0},{256,128},{384,256},{1,385},{129,1},{257,129},{385... | collective-permute-start | bytes 49160 | tf_op jit(solution)/shard_map/ppermute | solution.py:288
  41.9 2.5 %collective-permute-start.1 = (f32[32,128]{1,0:T(8,128)S(1)}, f32[32,128]{1,0:T(8,128)S(1)}, u32[]{:S(2)}, u32[]{:S(2)}) collective-permute-start(f32[32,128]{1,0:T(8,128)S(1)} %bitcast.15), channel_id=1, source_target_pairs={{0,256},{128,384},{256,0},{384,128},{1,257},{129,385},{257,1},{385... | collective-permute-start | bytes 49160 | tf_op jit(solution)/shard_map/ppermute | solution.py:288
  44.4 2.5 %collective-permute-start = (f32[32,128]{1,0:T(8,128)S(1)}, f32[32,128]{1,0:T(8,128)S(1)}, u32[]{:S(2)}, u32[]{:S(2)}) collective-permute-start(f32[32,128]{1,0:T(8,128)S(1)} %bitcast.16), channel_id=1, source_target_pairs={{0,128},{128,256},{256,384},{384,0},{1,129},{129,257},{257,385},{3... | collective-permute-start | bytes 49160 | tf_op jit(solution)/shard_map/ppermute | solution.py:288
  46.9 3.7 %collective-permute-done = f32[32,128]{1,0:T(8,128)S(1)} collective-permute-done((f32[32,128]{1,0:T(8,128)S(1)}, f32[32,128]{1,0:T(8,128)S(1)}, u32[]{:S(2)}, u32[]{:S(2)}) %collective-permute-start) | collective-permute-done | bytes 16416 | tf_op jit(solution)/shard_map/ppermute | solution.py:288
  50.7 0.0 collective-permute-done.1
  50.7 0.0 collective-permute-done.2
  50.7 2.8 %collective-permute-start.3 = (f32[128,128]{1,0:T(8,128)S(1)}, f32[128,128]{1,0:T(8,128)S(1)}, u32[]{:S(2)}, u32[]{:S(2)}) collective-permute-start(f32[128,128]{1,0:T(8,128)S(1)} %get-tuple-element.13), channel_id=1, source_target_pairs={{0,8},{8,16},{16,24},{24,0},{1,9},{9,17},{17,25},{25,1},{2,10},{10... | collective-permute-start | bytes 196616 | tf_op jit(solution)/shard_map/ppermute | solution.py:288
  53.5 0.1 pad_add_fusion.place_ref
  53.6 3.6 %collective-permute-start.5 = (f32[128,128]{1,0:T(8,128)S(1)}, f32[128,128]{1,0:T(8,128)S(1)}, u32[]{:S(2)}, u32[]{:S(2)}) collective-permute-start(f32[128,128]{1,0:T(8,128)S(1)} %get-tuple-element.13), channel_id=1, source_target_pairs={{0,24},{8,0},{16,8},{24,16},{1,25},{9,1},{17,9},{25,17},{2,26},{10... | collective-permute-start | bytes 196616 | tf_op jit(solution)/shard_map/ppermute | solution.py:288
  57.3 3.2 %collective-permute-start.4 = (f32[128,128]{1,0:T(8,128)S(1)}, f32[128,128]{1,0:T(8,128)S(1)}, u32[]{:S(2)}, u32[]{:S(2)}) collective-permute-start(f32[128,128]{1,0:T(8,128)S(1)} %get-tuple-element.13), channel_id=1, source_target_pairs={{0,16},{8,24},{16,0},{24,8},{1,17},{9,25},{17,1},{25,9},{2,18},{10... | collective-permute-start | bytes 196616 | tf_op jit(solution)/shard_map/ppermute | solution.py:288
  60.4 0.0 collective-permute-done.3
  60.5 4.0 %collective-permute-done.4 = f32[128,128]{1,0:T(8,128)S(1)} collective-permute-done((f32[128,128]{1,0:T(8,128)S(1)}, f32[128,128]{1,0:T(8,128)S(1)}, u32[]{:S(2)}, u32[]{:S(2)}) %collective-permute-start.4) | collective-permute-done | bytes 65568 | tf_op jit(solution)/shard_map/ppermute | solution.py:288
  64.4 0.0 collective-permute-done.5
  64.5 2.0 %prepare.1 = (bf16[512,512]{1,0:T(8,128)(2,1)S(1)}, f32[512,512]{1,0:T(8,128)S(1)}) custom-call(f32[512,128]{1,0:T(8,128)S(1)} %constant_dynamic-update-slice_fusion.4.tile_ref, s32[2]{0:T(128)S(1)} %pad_add_fusion.place_ref), custom_call_target="tpu_custom_call" | custom-call | tf_op jit(solution)/shard_map/prepare/pallas_call | solution.py:206
  66.4 27.4 %all-to-all-done.1 = bf16[512,8,128]{2,1,0:T(8,128)(2,1)S(1)} async-done(((bf16[512,8,128]{2,1,0:T(8,128)(2,1)}), bf16[512,8,128]{2,1,0:T(8,128)(2,1)S(1)}, u32[]{:S(2)}, u32[]{:S(2)}) %all-to-all-start.1) | async-done | bytes 1048608 | tf_op jit(solution)/shard_map/all_to_all | solution.py:300
  93.9 3.1 %correlate.1 = bf16[4,512,512]{2,1,0:T(8,128)(2,1)} custom-call(bf16[4096,128]{1,0:T(8,128)(2,1)S(1)} %bitcast.11, bf16[512,512]{1,0:T(8,128)(2,1)S(1)} %get-tuple-element.11.sel_ref, f32[512,512]{1,0:T(8,128)S(1)} %get-tuple-element.12.inv_ref), custom_call_target="tpu_custom_call" | custom-call | tf_op jit(solution)/shard_map/correlate/pallas_call | solution.py:251
  (7 shorter events, 0.0 us)
Async XLA Ops:
  1.4 14.4 %all-to-all-start = ((f32[4,8,128]{2,1,0:T(8,128)}), f32[4,8,128]{2,1,0:T(8,128)S(1)}, u32[]{:S(2)}, u32[]{:S(2)}) async-start(f32[4,8,128]{2,1,0:T(8,128)} %make_tiles.1), calls=%async_computation | async-start | bytes 32768 | tf_op jit(solution)/shard_map/all_to_all | solution.py:297
  15.8 78.1 %all-to-all-start.1 = ((bf16[512,8,128]{2,1,0:T(8,128)(2,1)}), bf16[512,8,128]{2,1,0:T(8,128)(2,1)S(1)}, u32[]{:S(2)}, u32[]{:S(2)}) async-start(bf16[512,8,128]{2,1,0:T(8,128)(2,1)} %bitcast.12), calls=%async_computation.1 | async-start | bytes 2097152 | tf_op jit(solution)/shard_map/all_to_all | solution.py:300
  37.4 13.2 %collective-permute-start.2 = (f32[32,128]{1,0:T(8,128)S(1)}, f32[32,128]{1,0:T(8,128)S(1)}, u32[]{:S(2)}, u32[]{:S(2)}) collective-permute-start(f32[32,128]{1,0:T(8,128)S(1)} %bitcast.14), channel_id=1, source_target_pairs={{0,384},{128,0},{256,128},{384,256},{1,385},{129,1},{257,129},{385... | collective-permute-start | bytes 49160 | tf_op jit(solution)/shard_map/ppermute | solution.py:288
  41.9 8.7 %collective-permute-start.1 = (f32[32,128]{1,0:T(8,128)S(1)}, f32[32,128]{1,0:T(8,128)S(1)}, u32[]{:S(2)}, u32[]{:S(2)}) collective-permute-start(f32[32,128]{1,0:T(8,128)S(1)} %bitcast.15), channel_id=1, source_target_pairs={{0,256},{128,384},{256,0},{384,128},{1,257},{129,385},{257,1},{385... | collective-permute-start | bytes 49160 | tf_op jit(solution)/shard_map/ppermute | solution.py:288
  44.4 6.2 %collective-permute-start = (f32[32,128]{1,0:T(8,128)S(1)}, f32[32,128]{1,0:T(8,128)S(1)}, u32[]{:S(2)}, u32[]{:S(2)}) collective-permute-start(f32[32,128]{1,0:T(8,128)S(1)} %bitcast.16), channel_id=1, source_target_pairs={{0,128},{128,256},{256,384},{384,0},{1,129},{129,257},{257,385},{3... | collective-permute-start | bytes 49160 | tf_op jit(solution)/shard_map/ppermute | solution.py:288
  50.7 9.8 %collective-permute-start.3 = (f32[128,128]{1,0:T(8,128)S(1)}, f32[128,128]{1,0:T(8,128)S(1)}, u32[]{:S(2)}, u32[]{:S(2)}) collective-permute-start(f32[128,128]{1,0:T(8,128)S(1)} %get-tuple-element.13), channel_id=1, source_target_pairs={{0,8},{8,16},{16,24},{24,0},{1,9},{9,17},{17,25},{25,1},{2,10},{10... | collective-permute-start | bytes 196616 | tf_op jit(solution)/shard_map/ppermute | solution.py:288
  53.6 10.8 %collective-permute-start.5 = (f32[128,128]{1,0:T(8,128)S(1)}, f32[128,128]{1,0:T(8,128)S(1)}, u32[]{:S(2)}, u32[]{:S(2)}) collective-permute-start(f32[128,128]{1,0:T(8,128)S(1)} %get-tuple-element.13), channel_id=1, source_target_pairs={{0,24},{8,0},{16,8},{24,16},{1,25},{9,1},{17,9},{25,17},{2,26},{10... | collective-permute-start | bytes 196616 | tf_op jit(solution)/shard_map/ppermute | solution.py:288
  57.3 7.2 %collective-permute-start.4 = (f32[128,128]{1,0:T(8,128)S(1)}, f32[128,128]{1,0:T(8,128)S(1)}, u32[]{:S(2)}, u32[]{:S(2)}) collective-permute-start(f32[128,128]{1,0:T(8,128)S(1)} %get-tuple-element.13), channel_id=1, source_target_pairs={{0,16},{8,24},{16,0},{24,8},{1,17},{9,25},{17,1},{25,9},{2,18},{10... | collective-permute-start | bytes 196616 | tf_op jit(solution)/shard_map/ppermute | solution.py:288

commit v8 on v7

--- a/solution.py
+++ b/solution.py
@@ -131,13 +131,17 @@
     weight = w_ref[pl.ds(z_ref[0], 1), :]
     dhi, dlo = dhi_ref[...], dlo_ref[...]
     for q in range(4):
+        starts = [2048 * (q % 2) + 1024 * a + 512 * (q // 2) for a in range(2)]
         for i in range(4):
             hi = ahi_ref[4 * q + i]
             out = dot(dhi, hi) + (dot(dhi, alo_ref[4 * q + i]) + dot(dlo, hi))
             out = out.astype(BF16).astype(F32) * weight
             for c in range(2):
-                m_ref[pl.ds(1024 * q + 2 * i + c, 128, stride=8), :] = out[128 * c : 128 * (c + 1)]
-        o_ref[1024 * q : 1024 * (q + 1), :] = m_ref[1024 * q : 1024 * (q + 1), :].astype(BF16)
+                for a in range(2):
+                    rows = out[128 * c + 64 * a : 128 * c + 64 * (a + 1)]
+                    m_ref[pl.ds(starts[a] + 2 * i + c, 64, stride=8), :] = rows
+        for start in starts:
+            o_ref[start : start + 512, :] = m_ref[start : start + 512, :].astype(BF16)
 
 
 def channelize(voltages, flags, station, spectra, interpret=False):
@@ -147,7 +151,7 @@
     h = np.repeat(filter_rows(taps, lanes).reshape(taps * 16, 128), 2, axis=0)
     tw = twist_rows(16, 128)
     d = inner_matrix(128, 1.0 / math.sqrt(lanes))
-    d = d.reshape(4, 4, 4, 2, 2, 256).transpose(4, 0, 2, 3, 1, 5).reshape(256, 256)
+    d = d.reshape(4, 4, 4, 2, 2, 256).transpose(4, 3, 1, 0, 2, 5).reshape(256, 256)
     dhi = d.astype(np.float32).astype(jnp.bfloat16)
     dlo = (d - dhi.astype(np.float64)).astype(np.float32).astype(jnp.bfloat16)
     tables = [jnp.asarray(x) for x in (h, tw, dhi, dlo)]
@@ -181,11 +185,11 @@
     lane = lax.broadcasted_iota(jnp.int32, (8, rows), 1)
     ids = jnp.where((lane & 7) < 4, ids, -1.0)
     down = lax.broadcasted_iota(jnp.int32, (rows, rows), 0)
-    pol = (lane >> 7) & 1
-    x = (place_ref[0] - ((lane >> 5) & 3)) & 3
-    y = (place_ref[1] - ((lane >> 3) & 3)) & 3
-    z = lane & 3
-    spot = y * 128 + x * 32 + z * 8 + ((lane >> 2) & 1) * 2 + (lane >> 8)
+    pol = lane >> 8
+    x = (place_ref[0] - ((lane >> 2) & 3)) & 3
+    y = (place_ref[1] - (lane & 3)) & 3
+    z = (lane >> 4) & 3
+    spot = y * 128 + x * 32 + z * 8 + ((lane >> 7) & 1) * 2 + ((lane >> 6) & 1)
     move = jnp.where(down == spot[0:1], 1.0, 0.0).astype(BF16)
     moved = jnp.dot(ids.astype(BF16), move, preferred_element_type=F32).astype(jnp.int32)
     source_row = 2 * moved + pol
@@ -297,7 +301,7 @@
     tile = lax.all_to_all(tile, "l", split_axis=0, concat_axis=0, tiled=True).reshape(32, spectra)
     blocks = channelize(frames, flags, z_hi, spectra).reshape(512, 8, spectra)
     tile, blocks = lax.optimization_barrier((tile, blocks))
-    moved = lax.all_to_all(blocks, ("b", "c", "x", "y", "a", "l"), split_axis=0, concat_axis=0, tiled=True)
+    moved = lax.all_to_all(blocks, ("c", "a", "b", "l", "x", "y"), split_axis=0, concat_axis=0, tiled=True)
     for axis in ("x", "y"):
         tile = gather_line(tile, axis)
     place = jnp.stack([lax.axis_index(axis) for axis in ("x", "y")]).astype(jnp.int32)

time: 97.4 us -> 96.9 us (level)
  no operation moved by 1% of the time
where the time goes in v8:
time: 96.9 us; the launch traced here: 96.3 us
  starting transfers between devices  47.2 us (49%)
  waiting for transfers between devices  34.5 us (36%)
  Pallas kernels  14.4 us (15%)
    all_to_all x1, waiting for transfers between devices, on_device(): lax.all_to_all(blocks, ('c', 'a', 'b', 'l', 'x', 'y'), split_axis=0, conc...  26.9 us
    all_to_all x1, starting transfers between devices, on_device(): lax.all_to_all(blocks, ('c', 'a', 'b', 'l', 'x', 'y'), split_axis=0, conc...  21.6 us
    ppermute x6, starting transfers between devices, gather_line(): lax.ppermute(tile, axis, [(i, (i + shift) % 4) for i in range(4)])  19.1 us
    pallas_call x1, Pallas kernels, channelize(): pl.pallas_call(channelize_kernel, out_shape=jax.ShapeDtypeStruct((4096, s...  7.95 us
    ppermute x6, waiting for transfers between devices, gather_line(): lax.ppermute(tile, axis, [(i, (i + shift) % 4) for i in range(4)])  7.61 us
    all_to_all x1, starting transfers between devices, on_device(): lax.all_to_all(tile, 'l', split_axis=0, concat_axis=0, tiled=True)  6.43 us
    pallas_call x1, Pallas kernels, correlate(): pl.pallas_call(correlate_kernel, grid=(channels // 2,), in_specs=[pl.Bloc...  3.08 us
    pallas_call x1, Pallas kernels, prepare(): pl.pallas_call(prepare_kernel, out_shape=(jax.ShapeDtypeStruct((inputs, i...  1.97 us
  transfers between devices with their start and end apart: 8, of which 3 were waited for; matrix products, arithmetic and copies ran while one was open for 0% of the time, Pallas kernels for 10%

profile of v8, /device:TPU:1, one launch (start us, length us, event | category | flops | bytes accessed | tf_op | source)
XLA Modules:
  0.0 96.3 jit_solution(14021824751657403620)
XLA Ops:
  0.0 1.4 %make_tiles.1 = f32[4,8,128]{2,1,0:T(8,128)} custom-call(f32[4,128]{1,0:T(4,128)} %w_ref.1, s32[4]{0:T(128)} %row_ref.1), custom_call_target="tpu_custom_call" | custom-call | tf_op jit(solution)/shard_map/make_tiles/pallas_call | solution.py:280
  1.4 6.4 %all-to-all-start = ((f32[4,8,128]{2,1,0:T(8,128)}), f32[4,8,128]{2,1,0:T(8,128)S(1)}, u32[]{:S(2)}, u32[]{:S(2)}) async-start(f32[4,8,128]{2,1,0:T(8,128)} %make_tiles.1), calls=%async_computation | async-start | bytes 32768 | tf_op jit(solution)/shard_map/all_to_all | solution.py:301
  7.8 7.9 %channelize.1 = bf16[4096,128]{1,0:T(8,128)(2,1)} custom-call(bf16[4576,128]{1,0:T(8,128)(2,1)} %bitcast.13, f32[512,128]{1,0:T(8,128)} %constant.26.clone.h_ref, f32[2,16,128]{2,1,0:T(8,128)} %constant.27.clone.tw_ref, bf16[256,256]{1,0:T(8,128)(2,1)} %constant.28.clone.dhi_ref, bf16[256,256]{1,0:T(8,128)(2,1)} %constant.29.clone.dlo_ref, f32[4,128]{1,0:T(4,128)} %w_ref.1, ...), custom_call_target="tpu_custom_call" | custom-call | tf_op jit(solution)/shard_map/channelize/pallas_call | solution.py:158
  15.8 0.0 all-to-all-done
  15.8 21.6 %all-to-all-start.1 = ((bf16[512,8,128]{2,1,0:T(8,128)(2,1)}), bf16[512,8,128]{2,1,0:T(8,128)(2,1)S(1)}, u32[]{:S(2)}, u32[]{:S(2)}) async-start(bf16[512,8,128]{2,1,0:T(8,128)(2,1)} %bitcast.12), calls=%async_computation.1 | async-start | bytes 2097152 | tf_op jit(solution)/shard_map/all_to_all | solution.py:304
  37.4 4.5 %collective-permute-start.2 = (f32[32,128]{1,0:T(8,128)S(1)}, f32[32,128]{1,0:T(8,128)S(1)}, u32[]{:S(2)}, u32[]{:S(2)}) collective-permute-start(f32[32,128]{1,0:T(8,128)S(1)} %bitcast.14), channel_id=1, source_target_pairs={{0,384},{128,0},{256,128},{384,256},{1,385},{129,1},{257,129},{385... | collective-permute-start | bytes 49160 | tf_op jit(solution)/shard_map/ppermute | solution.py:292
  41.9 2.5 %collective-permute-start.1 = (f32[32,128]{1,0:T(8,128)S(1)}, f32[32,128]{1,0:T(8,128)S(1)}, u32[]{:S(2)}, u32[]{:S(2)}) collective-permute-start(f32[32,128]{1,0:T(8,128)S(1)} %bitcast.15), channel_id=1, source_target_pairs={{0,256},{128,384},{256,0},{384,128},{1,257},{129,385},{257,1},{385... | collective-permute-start | bytes 49160 | tf_op jit(solution)/shard_map/ppermute | solution.py:292
  44.4 2.5 %collective-permute-start = (f32[32,128]{1,0:T(8,128)S(1)}, f32[32,128]{1,0:T(8,128)S(1)}, u32[]{:S(2)}, u32[]{:S(2)}) collective-permute-start(f32[32,128]{1,0:T(8,128)S(1)} %bitcast.16), channel_id=1, source_target_pairs={{0,128},{128,256},{256,384},{384,0},{1,129},{129,257},{257,385},{3... | collective-permute-start | bytes 49160 | tf_op jit(solution)/shard_map/ppermute | solution.py:292
  46.9 3.7 %collective-permute-done = f32[32,128]{1,0:T(8,128)S(1)} collective-permute-done((f32[32,128]{1,0:T(8,128)S(1)}, f32[32,128]{1,0:T(8,128)S(1)}, u32[]{:S(2)}, u32[]{:S(2)}) %collective-permute-start) | collective-permute-done | bytes 16416 | tf_op jit(solution)/shard_map/ppermute | solution.py:292
  50.7 0.0 collective-permute-done.1
  50.7 0.0 collective-permute-done.2
  50.7 2.9 %collective-permute-start.3 = (f32[128,128]{1,0:T(8,128)S(1)}, f32[128,128]{1,0:T(8,128)S(1)}, u32[]{:S(2)}, u32[]{:S(2)}) collective-permute-start(f32[128,128]{1,0:T(8,128)S(1)} %get-tuple-element.13), channel_id=1, source_target_pairs={{0,8},{8,16},{16,24},{24,0},{1,9},{9,17},{17,25},{25,1},{2,10},{10... | collective-permute-start | bytes 196616 | tf_op jit(solution)/shard_map/ppermute | solution.py:292
  53.6 0.1 pad_add_fusion.place_ref
  53.7 3.6 %collective-permute-start.5 = (f32[128,128]{1,0:T(8,128)S(1)}, f32[128,128]{1,0:T(8,128)S(1)}, u32[]{:S(2)}, u32[]{:S(2)}) collective-permute-start(f32[128,128]{1,0:T(8,128)S(1)} %get-tuple-element.13), channel_id=1, source_target_pairs={{0,24},{8,0},{16,8},{24,16},{1,25},{9,1},{17,9},{25,17},{2,26},{10... | collective-permute-start | bytes 196616 | tf_op jit(solution)/shard_map/ppermute | solution.py:292
  57.3 3.2 %collective-permute-start.4 = (f32[128,128]{1,0:T(8,128)S(1)}, f32[128,128]{1,0:T(8,128)S(1)}, u32[]{:S(2)}, u32[]{:S(2)}) collective-permute-start(f32[128,128]{1,0:T(8,128)S(1)} %get-tuple-element.13), channel_id=1, source_target_pairs={{0,16},{8,24},{16,0},{24,8},{1,17},{9,25},{17,1},{25,9},{2,18},{10... | collective-permute-start | bytes 196616 | tf_op jit(solution)/shard_map/ppermute | solution.py:292
  60.4 0.0 collective-permute-done.3
  60.5 3.9 %collective-permute-done.4 = f32[128,128]{1,0:T(8,128)S(1)} collective-permute-done((f32[128,128]{1,0:T(8,128)S(1)}, f32[128,128]{1,0:T(8,128)S(1)}, u32[]{:S(2)}, u32[]{:S(2)}) %collective-permute-start.4) | collective-permute-done | bytes 65568 | tf_op jit(solution)/shard_map/ppermute | solution.py:292
  64.3 0.0 collective-permute-done.5
  64.4 2.0 %prepare.1 = (bf16[512,512]{1,0:T(8,128)(2,1)S(1)}, f32[512,512]{1,0:T(8,128)S(1)}) custom-call(f32[512,128]{1,0:T(8,128)S(1)} %constant_dynamic-update-slice_fusion.4.tile_ref, s32[2]{0:T(128)S(1)} %pad_add_fusion.place_ref), custom_call_target="tpu_custom_call" | custom-call | tf_op jit(solution)/shard_map/prepare/pallas_call | solution.py:210
  66.4 26.9 %all-to-all-done.1 = bf16[512,8,128]{2,1,0:T(8,128)(2,1)S(1)} async-done(((bf16[512,8,128]{2,1,0:T(8,128)(2,1)}), bf16[512,8,128]{2,1,0:T(8,128)(2,1)S(1)}, u32[]{:S(2)}, u32[]{:S(2)}) %all-to-all-start.1) | async-done | bytes 1048608 | tf_op jit(solution)/shard_map/all_to_all | solution.py:304
  93.2 3.1 %correlate.1 = bf16[4,512,512]{2,1,0:T(8,128)(2,1)} custom-call(bf16[4096,128]{1,0:T(8,128)(2,1)S(1)} %bitcast.11, bf16[512,512]{1,0:T(8,128)(2,1)S(1)} %get-tuple-element.11.sel_ref, f32[512,512]{1,0:T(8,128)S(1)} %get-tuple-element.12.inv_ref), custom_call_target="tpu_custom_call" | custom-call | tf_op jit(solution)/shard_map/correlate/pallas_call | solution.py:255
  (7 shorter events, 0.0 us)
Async XLA Ops:
  1.4 14.4 %all-to-all-start = ((f32[4,8,128]{2,1,0:T(8,128)}), f32[4,8,128]{2,1,0:T(8,128)S(1)}, u32[]{:S(2)}, u32[]{:S(2)}) async-start(f32[4,8,128]{2,1,0:T(8,128)} %make_tiles.1), calls=%async_computation | async-start | bytes 32768 | tf_op jit(solution)/shard_map/all_to_all | solution.py:301
  15.8 77.4 %all-to-all-start.1 = ((bf16[512,8,128]{2,1,0:T(8,128)(2,1)}), bf16[512,8,128]{2,1,0:T(8,128)(2,1)S(1)}, u32[]{:S(2)}, u32[]{:S(2)}) async-start(bf16[512,8,128]{2,1,0:T(8,128)(2,1)} %bitcast.12), calls=%async_computation.1 | async-start | bytes 2097152 | tf_op jit(solution)/shard_map/all_to_all | solution.py:304
  37.4 13.2 %collective-permute-start.2 = (f32[32,128]{1,0:T(8,128)S(1)}, f32[32,128]{1,0:T(8,128)S(1)}, u32[]{:S(2)}, u32[]{:S(2)}) collective-permute-start(f32[32,128]{1,0:T(8,128)S(1)} %bitcast.14), channel_id=1, source_target_pairs={{0,384},{128,0},{256,128},{384,256},{1,385},{129,1},{257,129},{385... | collective-permute-start | bytes 49160 | tf_op jit(solution)/shard_map/ppermute | solution.py:292
  41.9 8.7 %collective-permute-start.1 = (f32[32,128]{1,0:T(8,128)S(1)}, f32[32,128]{1,0:T(8,128)S(1)}, u32[]{:S(2)}, u32[]{:S(2)}) collective-permute-start(f32[32,128]{1,0:T(8,128)S(1)} %bitcast.15), channel_id=1, source_target_pairs={{0,256},{128,384},{256,0},{384,128},{1,257},{129,385},{257,1},{385... | collective-permute-start | bytes 49160 | tf_op jit(solution)/shard_map/ppermute | solution.py:292
  44.4 6.2 %collective-permute-start = (f32[32,128]{1,0:T(8,128)S(1)}, f32[32,128]{1,0:T(8,128)S(1)}, u32[]{:S(2)}, u32[]{:S(2)}) collective-permute-start(f32[32,128]{1,0:T(8,128)S(1)} %bitcast.16), channel_id=1, source_target_pairs={{0,128},{128,256},{256,384},{384,0},{1,129},{129,257},{257,385},{3... | collective-permute-start | bytes 49160 | tf_op jit(solution)/shard_map/ppermute | solution.py:292
  50.7 9.8 %collective-permute-start.3 = (f32[128,128]{1,0:T(8,128)S(1)}, f32[128,128]{1,0:T(8,128)S(1)}, u32[]{:S(2)}, u32[]{:S(2)}) collective-permute-start(f32[128,128]{1,0:T(8,128)S(1)} %get-tuple-element.13), channel_id=1, source_target_pairs={{0,8},{8,16},{16,24},{24,0},{1,9},{9,17},{17,25},{25,1},{2,10},{10... | collective-permute-start | bytes 196616 | tf_op jit(solution)/shard_map/ppermute | solution.py:292
  53.7 10.7 %collective-permute-start.5 = (f32[128,128]{1,0:T(8,128)S(1)}, f32[128,128]{1,0:T(8,128)S(1)}, u32[]{:S(2)}, u32[]{:S(2)}) collective-permute-start(f32[128,128]{1,0:T(8,128)S(1)} %get-tuple-element.13), channel_id=1, source_target_pairs={{0,24},{8,0},{16,8},{24,16},{1,25},{9,1},{17,9},{25,17},{2,26},{10... | collective-permute-start | bytes 196616 | tf_op jit(solution)/shard_map/ppermute | solution.py:292
  57.3 7.1 %collective-permute-start.4 = (f32[128,128]{1,0:T(8,128)S(1)}, f32[128,128]{1,0:T(8,128)S(1)}, u32[]{:S(2)}, u32[]{:S(2)}) collective-permute-start(f32[128,128]{1,0:T(8,128)S(1)} %get-tuple-element.13), channel_id=1, source_target_pairs={{0,16},{8,24},{16,0},{24,8},{1,17},{9,25},{17,1},{25,9},{2,18},{10... | collective-permute-start | bytes 196616 | tf_op jit(solution)/shard_map/ppermute | solution.py:292
